TPU v7x, 512 devices: a whole 4x8x8 slice. The times are simulated.
512 devices in a mesh: orb: 128 (over z, y, core), grid: 4 (over x).
Axes of the slice: x: 4, y: 8, z: 8, core: 2. Of those that a mesh axis runs over, the one named last changes fastest.
Arguments:
- orbitals: float32 [256, 32, 1024], P('orb', 'grid'), may hold values from -6 to 6
- dielectric: float32 [256, 32, 1024], P('orb', 'grid'), may hold values from 1 to 80
- pair_offsets: int32 [256, 4], replicated, may hold values from 0 to 3, each once within a row
- pair_counts: int32 [256], replicated, may hold values from 1 to 4, as said below
- box_shift: int32 [256], replicated, may hold values from 0 to 8
Outputs:
- exchange_action: float32 [256, 32, 1024], P('orb', 'grid')
Inputs may be any that keep to these rules, and one draw needn't show every extreme that they name: `pair_counts`: in each aligned block of 8 orbitals the counts sum to 16, and in each such block the 2 orbitals of one owner (an aligned run of 2 orbitals) all have 4. `pair_offsets`: each row is a permutation of 0 to 3; only its first pair_counts entries name pairs.
All inputs are finite; a program needn't handle non-finite values.
Results may differ from a plain program's by a relative error of at most 0.00013.
Values sent between devices are 32-bit elements; how exact they have to be, the bound alone decides.
No kernel may reach another device: no remote copies, remote signals or barrier semaphores. Data moves between devices by JAX's collectives and lax.ppermute only.
A program may use at most 64 MiB of HBM per device.

v0:
```python
import jax
import jax.numpy as jnp
from jax import lax
from jax.sharding import PartitionSpec as P

B = 32
PMAX = 4
SMAX = 8
CYCLES = 2
SWEEPS = 4


FOURPI = 4.0 * 3.141592653589793
OMEGA = 0.8
HIGHEST = lax.Precision.HIGHEST


def extended_2(value, sides, width):
    for axis, dim in sides:
        size, length = (lax.axis_size(axis), value.shape[dim])
        up = [(i, (i + 1) % size) for i in range(size - 1)]
        down = [(j, i) for i, j in up]
        last = lax.slice_in_dim(value, length - width, length, axis=dim)
        initial = lax.slice_in_dim(value, 0, width, axis=dim)
        before = lax.ppermute(last, axis, up)
        after = lax.ppermute(initial, axis, down)
        value = jnp.concatenate([before, value, after], axis=dim)
    return value


def passed_along(value, axis, steps):
    count = lax.axis_size(axis)
    pairs = [(source, (source + steps) % count) for source in range(count)]
    return lax.ppermute(value, axis, pairs)


def lookup(table, wanted):
    matches = wanted[:, None] == jnp.arange(table.shape[0], dtype=jnp.int32)[None, :]
    return jnp.sum(jnp.where(matches, table[None, :], 0), axis=1)


def beside_all(extended, edge_cells):
    centre = extended[:, 1:-1]
    column = lax.broadcasted_iota(jnp.int32, centre.shape, 2) % edge_cells
    row_padded = jnp.pad(centre, ((0, 0), (0, 0), (edge_cells, edge_cells)))
    col_padded = jnp.pad(centre, ((0, 0), (0, 0), (1, 1)))
    nothing = jnp.zeros_like(centre)
    neighbours = [
        extended[:, 2:],
        extended[:, :-2],
        row_padded[:, :, 2 * edge_cells :],
        row_padded[:, :, : -2 * edge_cells],
        jnp.where(column < edge_cells - 1, col_padded[:, :, 2:], nothing),
        jnp.where(column > 0, col_padded[:, :, :-2], nothing),
    ]
    return (centre, neighbours)


def diagonal_of(eps_ext, edge_cells, level_scale):
    centre, neighbours = beside_all(eps_ext, edge_cells)
    summed = jnp.zeros_like(centre)
    for eps_next in neighbours:
        summed = summed + 0.5 * (centre + eps_next)
    return level_scale * summed


def operate(values, level_data):
    eps_ext, diagonal, edge_cells, level_scale, whole_box = level_data
    extended = extended_2(values, (("grid", 1),), 1)
    neighbours = beside_all(extended, edge_cells)[1]
    eps_parts = beside_all(eps_ext, edge_cells)
    weighted = jnp.zeros_like(values)
    for eps_next, val_next in zip(eps_parts[1], neighbours):
        weighted = weighted + 0.5 * (eps_parts[0] + eps_next) * val_next
    return diagonal * values - level_scale * weighted


def coarsen(values, edge_cells):
    slot_count, layer_count, plane_cells = values.shape
    half_edge = edge_cells // 2
    grouped = values.reshape(slot_count, layer_count // 2, 2, half_edge, 2, half_edge, 2)
    return grouped.mean(axis=(2, 4, 6)).reshape(slot_count, layer_count // 2, plane_cells // 4)


def refine(values, half_edge):
    slot_count, layer_count, plane_cells = values.shape
    grown = jnp.broadcast_to(
        values.reshape(slot_count, layer_count, 1, half_edge, 1, half_edge, 1),
        (slot_count, layer_count, 2, half_edge, 2, half_edge, 2),
    )
    return grown.reshape(slot_count, 2 * layer_count, 4 * plane_cells)


def relaxed_step(values, rhs_level, level_data):
    diagonal = level_data[1]
    if values is None:
        return OMEGA * rhs_level / diagonal
    return values + OMEGA * (rhs_level - operate(values, level_data)) / diagonal


def multigrid_cycle(depth_index, values, rhs_level, levels):
    level_data = levels[depth_index]
    if depth_index == len(levels) - 1:
        for sweep_index in range(SWEEPS):
            values = relaxed_step(values, rhs_level, level_data)
        return values
    values = relaxed_step(values, rhs_level, level_data)
    residual = rhs_level - operate(values, level_data)
    correction = multigrid_cycle(depth_index + 1, None, coarsen(residual, level_data[2]), levels)
    values = values + refine(correction, level_data[2] // 2)
    return relaxed_step(values, rhs_level, level_data)


def shift_rows(values, row_offset, edge_cells):
    margin_cells = SMAX * edge_cells
    padded = jnp.pad(values, ((0, 0), (0, 0), (margin_cells, margin_cells)))
    plane_cells = values.shape[2]

    def one_slot(single, offset_value):
        return lax.dynamic_slice_in_dim(single, (SMAX + offset_value) * edge_cells, plane_cells, 1)

    return jax.vmap(one_slot)(padded, row_offset)


def solve_pairs(phi_first, second_field, eps_levels, row_offset, live_mask):
    moved = shift_rows(second_field, row_offset, B)
    rhs_fine = FOURPI * (phi_first * moved)
    levels = []
    for level_index in range(3):
        edge_cells = B // 2**level_index
        level_scale = 0.25**level_index
        eps_ext = eps_levels[level_index]
        levels.append(
            (eps_ext, diagonal_of(eps_ext, edge_cells, level_scale), edge_cells, level_scale, False)
        )
    potential = None
    for cycle_index in range(CYCLES):
        potential = multigrid_cycle(0, potential, rhs_fine, levels)
    to_first = -(potential * moved) * live_mask[:, None, None]
    to_second = -shift_rows(potential * phi_first, -row_offset, B) * live_mask[:, None, None]
    return (to_first, to_second)


def shards(orbitals, dielectric, pair_offsets, pair_counts, box_shift):
    owner = lax.axis_index("orb")
    orbital_count = pair_counts.shape[0]
    own_count = orbitals.shape[0]
    deep_rims = extended_2(dielectric, (("grid", 1),), 4)
    eps_fine = deep_rims[:, 3:-3]
    eps_half_deep = coarsen(deep_rims, B)
    eps_quarter = coarsen(eps_half_deep, B // 2)
    eps_half = eps_half_deep[:, 1:-1]
    own_fields = [orbitals, eps_fine, eps_half, eps_quarter]
    field_shapes = [item.shape[1:] for item in own_fields]
    field_sizes = [shape_pair[0] * shape_pair[1] for shape_pair in field_shapes]
    packet = jnp.concatenate([item.reshape(own_count, -1) for item in own_fields], axis=1)
    reach = (PMAX + own_count - 1) // own_count
    lowest = 0
    first_orb = owner * own_count + jnp.repeat(jnp.arange(own_count, dtype=jnp.int32), PMAX)
    pair_rank = jnp.tile(jnp.arange(PMAX, dtype=jnp.int32), own_count)
    live_mask = (pair_rank < lookup(pair_counts, first_orb)).astype(jnp.float32)
    slot_count = first_orb.shape[0]
    distance = 1 + lookup(pair_offsets.reshape(-1), first_orb * PMAX + pair_rank)
    second_orb = (first_orb + distance) % orbital_count
    row_offset = lookup(box_shift, first_orb) - lookup(box_shift, second_orb)
    window_first = (owner + lowest) * own_count
    first_place = (first_orb - window_first) % orbital_count
    second_place = (second_orb - window_first) % orbital_count
    arrived = []
    for offset in range(lowest, reach + 1):
        if offset == 0:
            arrived.append(packet)
        else:
            arrived.append(passed_along(packet, "orb", -offset))
    lane_index = jnp.arange(own_count, dtype=jnp.int32)
    first_fields = [
        jnp.zeros((slot_count,) + tuple(shape_pair), jnp.float32) for shape_pair in field_shapes
    ]
    second_field = jnp.zeros((slot_count,) + tuple(field_shapes[0]), jnp.float32)
    first_hots = []
    second_hots = []
    for block_index in range(reach - lowest + 1):
        targets = block_index * own_count + lane_index
        first_hot = (first_place[:, None] == targets[None, :]).astype(jnp.float32)
        second_hot = (second_place[:, None] == targets[None, :]).astype(jnp.float32)
        first_hots.append(first_hot)
        second_hots.append(second_hot)
        received = arrived[block_index]
        column_start = 0
        for field_index in range(len(field_shapes)):
            portion = received[:, column_start : column_start + field_sizes[field_index]]
            portion = portion.reshape((own_count,) + tuple(field_shapes[field_index]))
            first_fields[field_index] = first_fields[field_index] + jnp.einsum(
                "sa,azf->szf", first_hot, portion, precision=HIGHEST
            )
            if field_index == 0:
                second_field = second_field + jnp.einsum(
                    "sa,azf->szf", second_hot, portion, precision=HIGHEST
                )
            column_start = column_start + field_sizes[field_index]
    phi_first, eps_fine_slots, eps_half_slots, eps_quarter_slots = first_fields
    to_first, to_second = solve_pairs(
        phi_first,
        second_field,
        [eps_fine_slots, eps_half_slots, eps_quarter_slots],
        row_offset,
        live_mask,
    )
    outgoing = []
    for block_index in range(reach - lowest + 1):
        outgoing.append(
            jnp.einsum("sa,szf->azf", first_hots[block_index], to_first, precision=HIGHEST)
            + jnp.einsum("sa,szf->azf", second_hots[block_index], to_second, precision=HIGHEST)
        )
    collected = outgoing[-lowest]
    for offset in range(lowest, reach + 1):
        if offset != 0:
            collected = collected + passed_along(outgoing[offset - lowest], "orb", offset)
    return collected


def solution(mesh):
    placed = (P("orb", "grid", None), P("orb", "grid", None), P(), P(), P())
    return jax.shard_map(
        shards, mesh=mesh, in_specs=placed, out_specs=P("orb", "grid", None), check_vma=False
    )
```

profile of v0, /device:TPU:1, one launch (start us, length us, event | category | flops | bytes accessed | tf_op | source)
XLA Modules:
  0.0 248.2 jit_solution(8046919244517795764)
XLA Ops:
  1.0 3.9 %collective-permute-start = (f32[2,4,1024]{2,0,1:T(2,128)S(1)}, f32[2,4,1024]{2,0,1:T(2,128)S(1)}, u32[]{:S(2)}, u32[]{:S(2)}) collective-permute-start(f32[2,4,1024]{2,0,1:T(2,128)S(1)} %copy.251), channel_id=1, source_target_pairs={{0,1},{1,2},{2,3},{4,5},{5,6},{6,7},{8,9},{9,10},{10,11},{12,13},{... | collective-permute-start | bytes 98312 | tf_op jit(solution)/shard_map/ppermute | solution.py:25
  12.9 9.8 %reshape.292 = f32[2,8,2,16,2,16,2]{6,5,4,3,2,1,0:T(8,128)} reshape(f32[2,16,1024]{2,1,0:T(8,128)S(1)} %copy.132) | data formatting | bytes 262144 | tf_op jit(solution)/shard_map/reshape | solution.py:81
  22.7 4.0 %reduce_sum.90 = f32[2,8,16,16]{3,2,1,0:T(8,128)S(1)} reduce(f32[2,8,2,16,2,16,2]{6,5,4,3,2,1,0:T(8,128)} %reshape.292, f32[]{:T(128)} %constant.205.clone.1), dimensions={2,4,6}, to_apply=%region_0.0 | reduce | flops 28672 | bytes 147460 | tf_op jit(solution)/shard_map/reduce_sum | solution.py:82
  27.5 6.1 %collective-permute-start.2 = (f32[2,20224]{1,0:T(2,128)S(1)}, f32[2,20224]{1,0:T(2,128)S(1)}, u32[]{:S(2)}, u32[]{:S(2)}) collective-permute-start(f32[2,20224]{1,0:T(2,128)S(1)} %pad_maximum_fusion.10), channel_id=1, source_target_pairs={{0,508},{4,0},{8,4},{12,8},{16,12},{20,16},{24,20},{28,24},{32,28}... | collective-permute-start | bytes 485384 | tf_op jit(solution)/shard_map/ppermute | solution.py:34
  33.6 10.3 %collective-permute-start.3 = (f32[2,20224]{1,0:T(2,128)S(1)}, f32[2,20224]{1,0:T(2,128)S(1)}, u32[]{:S(2)}, u32[]{:S(2)}) collective-permute-start(f32[2,20224]{1,0:T(2,128)S(1)} %pad_maximum_fusion.10), channel_id=1, source_target_pairs={{0,504},{4,508},{8,0},{12,4},{16,8},{20,12},{24,16},{28,20},{32,24... | collective-permute-start | bytes 485384 | tf_op jit(solution)/shard_map/ppermute | solution.py:34
  44.9 2.1 collective-permute-done.3
  47.4 17.1 %while.2 = (s32[]{:T(128)}, f32[8,8,1536]{2,0,1:T(8,128)S(1)}, s32[8,3]{0,1:T(4,128)S(1)}, f32[8,8,1024]{2,0,1:T(8,128)S(1)}, s32[]{:T(128)}, /*index=5*/s32[]{:T(128)}) while((s32[]{:T(128)}, f32[8,8,1536]{2,0,1:T(8,128)S(1)}, s32[8,3]{0,1:T(4,128)S(1)}, f32[8,8,1024]{2,0,1:T(8,128)S(1)}, s32[]{:T(128)}, /*index=5*/s32[]{:T(128)}) %tuple.93), condition=%wide.while_cond, body=%wide.while_body.sunk | while | flops 2 | bytes 131197 | solution.py:120
  48.1 1.3 constant_dynamic-slice_fusion.9
  50.2 1.3 constant_dynamic-slice_fusion.9
  52.3 1.3 constant_dynamic-slice_fusion.9
  54.5 1.3 constant_dynamic-slice_fusion.9
  56.6 1.3 constant_dynamic-slice_fusion.9
  58.7 1.3 constant_dynamic-slice_fusion.9
  60.9 1.3 constant_dynamic-slice_fusion.9
  63.0 1.3 constant_dynamic-slice_fusion.9
  68.7 5.2 %collective-permute-start.5 = (f32[8,1,1024]{2,0,1:T(8,128)S(1)}, f32[8,1,1024]{2,0,1:T(8,128)S(1)}, u32[]{:S(2)}, u32[]{:S(2)}) collective-permute-start(f32[8,1,1024]{2,0,1:T(8,128)S(1)} %get-tuple-element.125), channel_id=1, source_target_pairs={{0,1},{1,2},{2,3},{4,5},{5,6},{6,7},{8,9},{9,10},{10,11},{12,13},{... | collective-permute-start | bytes 98312 | tf_op jit(solution)/shard_map/ppermute | solution.py:25
  75.3 2.6 %copy.139 = f32[8,8,1024]{0,2,1:T(8,128)} copy(f32[8,8,1024]{2,0,1:T(8,128)S(1)} %fusion.25) | data formatting | bytes 524288 | tf_op jit(solution)/shard_map/sub | solution.py:108
  77.9 5.0 %reduce_sum.95 = f32[8,4,16,16]{0,3,2,1:T(8,128)S(1)} reduce(f32[8,4,2,16,2,16,2]{0,6,5,4,3,2,1:T(2,128)} %bitcast.124, f32[]{:T(128)} %constant.205.clone.1), dimensions={2,4,6}, to_apply=%region_5.6 | reduce | flops 57344 | bytes 294916 | tf_op jit(solution)/shard_map/reduce_sum | solution.py:82
  84.9 4.4 %collective-permute-start.7 = (f32[8,1,256]{2,0,1:T(8,128)S(1)}, f32[8,1,256]{2,0,1:T(8,128)S(1)}, u32[]{:S(2)}, u32[]{:S(2)}) collective-permute-start(f32[8,1,256]{2,0,1:T(8,128)S(1)} %get-tuple-element.139), channel_id=1, source_target_pairs={{0,1},{1,2},{2,3},{4,5},{5,6},{6,7},{8,9},{9,10},{10,11},{12,13},{... | collective-permute-start | bytes 24584 | tf_op jit(solution)/shard_map/ppermute | solution.py:25
  92.0 4.2 %collective-permute-start.9 = (f32[8,1,64]{2,0,1:T(8,128)S(1)}, f32[8,1,64]{2,0,1:T(8,128)S(1)}, u32[]{:S(2)}, u32[]{:S(2)}) collective-permute-start(f32[8,1,64]{2,0,1:T(8,128)S(1)} %get-tuple-element.151), channel_id=1, source_target_pairs={{0,1},{1,2},{2,3},{4,5},{5,6},{6,7},{8,9},{9,10},{10,11},{12,13},{... | collective-permute-start | bytes 6152 | tf_op jit(solution)/shard_map/ppermute | solution.py:25
  98.4 4.2 %collective-permute-start.11 = (f32[8,1,64]{2,0,1:T(8,128)S(1)}, f32[8,1,64]{2,0,1:T(8,128)S(1)}, u32[]{:S(2)}, u32[]{:S(2)}) collective-permute-start(f32[8,1,64]{2,0,1:T(8,128)S(1)} %get-tuple-element.149), channel_id=1, source_target_pairs={{0,1},{1,2},{2,3},{4,5},{5,6},{6,7},{8,9},{9,10},{10,11},{12,13},{... | collective-permute-start | bytes 6152 | tf_op jit(solution)/shard_map/ppermute | solution.py:25
  104.8 4.2 %collective-permute-start.13 = (f32[8,1,64]{2,0,1:T(8,128)S(1)}, f32[8,1,64]{2,0,1:T(8,128)S(1)}, u32[]{:S(2)}, u32[]{:S(2)}) collective-permute-start(f32[8,1,64]{2,0,1:T(8,128)S(1)} %get-tuple-element.147), channel_id=1, source_target_pairs={{0,1},{1,2},{2,3},{4,5},{5,6},{6,7},{8,9},{9,10},{10,11},{12,13},{... | collective-permute-start | bytes 6152 | tf_op jit(solution)/shard_map/ppermute | solution.py:25
  111.6 4.2 %collective-permute-start.15 = (f32[8,1,256]{2,0,1:T(8,128)S(1)}, f32[8,1,256]{2,0,1:T(8,128)S(1)}, u32[]{:S(2)}, u32[]{:S(2)}) collective-permute-start(f32[8,1,256]{2,0,1:T(8,128)S(1)} %get-tuple-element.137), channel_id=1, source_target_pairs={{0,1},{1,2},{2,3},{4,5},{5,6},{6,7},{8,9},{9,10},{10,11},{12,13},{... | collective-permute-start | bytes 24584 | tf_op jit(solution)/shard_map/ppermute | solution.py:25
  117.0 4.1 %broadcast_in_dim.133 = f32[8,4,2,16,2,16,2]{0,6,5,4,3,2,1:T(2,128)} broadcast(f32[8,4,16,16]{0,3,2,1:T(8,128)S(1)} %bitcast.128), dimensions={0,1,3,5} | broadcast | bytes 294912 | tf_op jit(solution)/shard_map/broadcast_in_dim | solution.py:87
  121.1 2.8 %copy.154 = f32[8,8,1024]{2,0,1:T(8,128)S(1)} copy(f32[8,8,1024]{0,2,1:T(8,128)} %bitcast.125) | data formatting | bytes 524288 | tf_op jit(solution)/shard_map/reshape | solution.py:91
  125.2 4.2 %collective-permute-start.17 = (f32[8,1,1024]{2,0,1:T(8,128)S(1)}, f32[8,1,1024]{2,0,1:T(8,128)S(1)}, u32[]{:S(2)}, u32[]{:S(2)}) collective-permute-start(f32[8,1,1024]{2,0,1:T(8,128)S(1)} %get-tuple-element.121), channel_id=1, source_target_pairs={{0,1},{1,2},{2,3},{4,5},{5,6},{6,7},{8,9},{9,10},{10,11},{12,13},{... | collective-permute-start | bytes 98312 | tf_op jit(solution)/shard_map/ppermute | solution.py:25
  132.2 4.3 %collective-permute-start.19 = (f32[8,1,1024]{2,0,1:T(8,128)S(1)}, f32[8,1,1024]{2,0,1:T(8,128)S(1)}, u32[]{:S(2)}, u32[]{:S(2)}) collective-permute-start(f32[8,1,1024]{2,0,1:T(8,128)S(1)} %get-tuple-element.119), channel_id=1, source_target_pairs={{0,1},{1,2},{2,3},{4,5},{5,6},{6,7},{8,9},{9,10},{10,11},{12,13},{... | collective-permute-start | bytes 98312 | tf_op jit(solution)/shard_map/ppermute | solution.py:25
  139.3 4.3 %collective-permute-start.21 = (f32[8,1,1024]{2,0,1:T(8,128)S(1)}, f32[8,1,1024]{2,0,1:T(8,128)S(1)}, u32[]{:S(2)}, u32[]{:S(2)}) collective-permute-start(f32[8,1,1024]{2,0,1:T(8,128)S(1)} %get-tuple-element.117), channel_id=1, source_target_pairs={{0,1},{1,2},{2,3},{4,5},{5,6},{6,7},{8,9},{9,10},{10,11},{12,13},{... | collective-permute-start | bytes 98312 | tf_op jit(solution)/shard_map/ppermute | solution.py:25
  144.9 2.6 %copy.155 = f32[8,8,1024]{0,2,1:T(8,128)} copy(f32[8,8,1024]{2,0,1:T(8,128)S(1)} %fusion.55) | data formatting | bytes 524288 | tf_op jit(solution)/shard_map/sub | solution.py:108
  147.6 5.0 %reduce_sum.97 = f32[8,4,16,16]{0,3,2,1:T(8,128)S(1)} reduce(f32[8,4,2,16,2,16,2]{0,6,5,4,3,2,1:T(2,128)} %bitcast.126, f32[]{:T(128)} %constant.205.clone.1), dimensions={2,4,6}, to_apply=%region_7.8 | reduce | flops 57344 | bytes 294916 | tf_op jit(solution)/shard_map/reduce_sum | solution.py:82
  154.4 4.3 %collective-permute-start.23 = (f32[8,1,256]{2,0,1:T(8,128)S(1)}, f32[8,1,256]{2,0,1:T(8,128)S(1)}, u32[]{:S(2)}, u32[]{:S(2)}) collective-permute-start(f32[8,1,256]{2,0,1:T(8,128)S(1)} %get-tuple-element.135), channel_id=1, source_target_pairs={{0,1},{1,2},{2,3},{4,5},{5,6},{6,7},{8,9},{9,10},{10,11},{12,13},{... | collective-permute-start | bytes 24584 | tf_op jit(solution)/shard_map/ppermute | solution.py:25
  161.5 4.2 %collective-permute-start.25 = (f32[8,1,64]{2,0,1:T(8,128)S(1)}, f32[8,1,64]{2,0,1:T(8,128)S(1)}, u32[]{:S(2)}, u32[]{:S(2)}) collective-permute-start(f32[8,1,64]{2,0,1:T(8,128)S(1)} %get-tuple-element.145), channel_id=1, source_target_pairs={{0,1},{1,2},{2,3},{4,5},{5,6},{6,7},{8,9},{9,10},{10,11},{12,13},{... | collective-permute-start | bytes 6152 | tf_op jit(solution)/shard_map/ppermute | solution.py:25
  167.9 4.2 %collective-permute-start.27 = (f32[8,1,64]{2,0,1:T(8,128)S(1)}, f32[8,1,64]{2,0,1:T(8,128)S(1)}, u32[]{:S(2)}, u32[]{:S(2)}) collective-permute-start(f32[8,1,64]{2,0,1:T(8,128)S(1)} %get-tuple-element.143), channel_id=1, source_target_pairs={{0,1},{1,2},{2,3},{4,5},{5,6},{6,7},{8,9},{9,10},{10,11},{12,13},{... | collective-permute-start | bytes 6152 | tf_op jit(solution)/shard_map/ppermute | solution.py:25
  174.3 4.2 %collective-permute-start.29 = (f32[8,1,64]{2,0,1:T(8,128)S(1)}, f32[8,1,64]{2,0,1:T(8,128)S(1)}, u32[]{:S(2)}, u32[]{:S(2)}) collective-permute-start(f32[8,1,64]{2,0,1:T(8,128)S(1)} %get-tuple-element.141), channel_id=1, source_target_pairs={{0,1},{1,2},{2,3},{4,5},{5,6},{6,7},{8,9},{9,10},{10,11},{12,13},{... | collective-permute-start | bytes 6152 | tf_op jit(solution)/shard_map/ppermute | solution.py:25
  181.1 4.2 %collective-permute-start.31 = (f32[8,1,256]{2,0,1:T(8,128)S(1)}, f32[8,1,256]{2,0,1:T(8,128)S(1)}, u32[]{:S(2)}, u32[]{:S(2)}) collective-permute-start(f32[8,1,256]{2,0,1:T(8,128)S(1)} %get-tuple-element.133), channel_id=1, source_target_pairs={{0,1},{1,2},{2,3},{4,5},{5,6},{6,7},{8,9},{9,10},{10,11},{12,13},{... | collective-permute-start | bytes 24584 | tf_op jit(solution)/shard_map/ppermute | solution.py:25
  186.4 4.1 %broadcast_in_dim.137 = f32[8,4,2,16,2,16,2]{0,6,5,4,3,2,1:T(2,128)} broadcast(f32[8,4,16,16]{0,3,2,1:T(8,128)S(1)} %bitcast.129), dimensions={0,1,3,5} | broadcast | bytes 294912 | tf_op jit(solution)/shard_map/broadcast_in_dim | solution.py:87
  190.6 2.8 %copy.167 = f32[8,8,1024]{2,0,1:T(8,128)S(1)} copy(f32[8,8,1024]{0,2,1:T(8,128)} %bitcast.127) | data formatting | bytes 524288 | tf_op jit(solution)/shard_map/reshape | solution.py:91
  194.7 4.2 %collective-permute-start.33 = (f32[8,1,1024]{2,0,1:T(8,128)S(1)}, f32[8,1,1024]{2,0,1:T(8,128)S(1)}, u32[]{:S(2)}, u32[]{:S(2)}) collective-permute-start(f32[8,1,1024]{2,0,1:T(8,128)S(1)} %get-tuple-element.113), channel_id=1, source_target_pairs={{0,1},{1,2},{2,3},{4,5},{5,6},{6,7},{8,9},{9,10},{10,11},{12,13},{... | collective-permute-start | bytes 98312 | tf_op jit(solution)/shard_map/ppermute | solution.py:25
  201.2 17.1 %while.3 = (s32[]{:T(128)}, f32[8,8,1536]{2,0,1:T(8,128)S(1)}, s32[8,3]{0,1:T(4,128)S(1)}, f32[8,8,1024]{2,0,1:T(8,128)S(1)}, s32[]{:T(128)}, /*index=5*/s32[]{:T(128)}) while((s32[]{:T(128)}, f32[8,8,1536]{2,0,1:T(8,128)S(1)}, s32[8,3]{0,1:T(4,128)S(1)}, f32[8,8,1024]{2,0,1:T(8,128)S(1)}, s32[]{:T(128)}, /*index=5*/s32[]{:T(128)}) %tuple.96), condition=%wide.while_cond.1, body=%wide.while_body.1.sunk | while | flops 2 | bytes 131197 | solution.py:120
  201.8 1.3 constant_dynamic-slice_fusion.11
  204.0 1.3 constant_dynamic-slice_fusion.11
  206.1 1.3 constant_dynamic-slice_fusion.11
  208.2 1.3 constant_dynamic-slice_fusion.11
  210.4 1.3 constant_dynamic-slice_fusion.11
  212.5 1.3 constant_dynamic-slice_fusion.11
  218.6 19.2 %collective-permute-start.34 = (f32[2,8,1024]{2,0,1:T(2,128)S(1)}, f32[2,8,1024]{2,0,1:T(2,128)S(1)}, u32[]{:S(2)}, u32[]{:S(2)}) collective-permute-start(f32[2,8,1024]{2,0,1:T(2,128)S(1)} %convolution_add_fusion.6), channel_id=1, source_target_pairs={{0,4},{4,8},{8,12},{12,16},{16,20},{20,24},{24,28},{28,32},{32,36}... | collective-permute-start | bytes 196616 | tf_op jit(solution)/shard_map/ppermute | solution.py:34
  238.1 1.9 collective-permute-start.35
  240.3 6.9 %collective-permute-done.35 = f32[2,8,1024]{2,0,1:T(2,128)S(1)} collective-permute-done((f32[2,8,1024]{2,0,1:T(2,128)S(1)}, f32[2,8,1024]{2,0,1:T(2,128)S(1)}, u32[]{:S(2)}, u32[]{:S(2)}) %collective-permute-start.35) | collective-permute-done | bytes 65568 | tf_op jit(solution)/shard_map/ppermute | solution.py:34
  (248 shorter events, 69.6 us)
Async XLA Ops:
  1.0 10.9 %collective-permute-start = (f32[2,4,1024]{2,0,1:T(2,128)S(1)}, f32[2,4,1024]{2,0,1:T(2,128)S(1)}, u32[]{:S(2)}, u32[]{:S(2)}) collective-permute-start(f32[2,4,1024]{2,0,1:T(2,128)S(1)} %copy.251), channel_id=1, source_target_pairs={{0,1},{1,2},{2,3},{4,5},{5,6},{6,7},{8,9},{9,10},{10,11},{12,13},{... | collective-permute-start | bytes 98312 | tf_op jit(solution)/shard_map/ppermute | solution.py:25
  4.9 7.8 %collective-permute-start.1 = (f32[2,4,1024]{2,0,1:T(2,128)S(1)}, f32[2,4,1024]{2,0,1:T(2,128)S(1)}, u32[]{:S(2)}, u32[]{:S(2)}) collective-permute-start(f32[2,4,1024]{2,0,1:T(2,128)S(1)} %copy.252), channel_id=1, source_target_pairs={{1,0},{2,1},{3,2},{5,4},{6,5},{7,6},{9,8},{10,9},{11,10},{13,12},{... | collective-permute-start | bytes 98312 | tf_op jit(solution)/shard_map/ppermute | solution.py:26
  27.5 17.0 %collective-permute-start.2 = (f32[2,20224]{1,0:T(2,128)S(1)}, f32[2,20224]{1,0:T(2,128)S(1)}, u32[]{:S(2)}, u32[]{:S(2)}) collective-permute-start(f32[2,20224]{1,0:T(2,128)S(1)} %pad_maximum_fusion.10), channel_id=1, source_target_pairs={{0,508},{4,0},{8,4},{12,8},{16,12},{20,16},{24,20},{28,24},{32,28}... | collective-permute-start | bytes 485384 | tf_op jit(solution)/shard_map/ppermute | solution.py:34
  33.6 13.3 %collective-permute-start.3 = (f32[2,20224]{1,0:T(2,128)S(1)}, f32[2,20224]{1,0:T(2,128)S(1)}, u32[]{:S(2)}, u32[]{:S(2)}) collective-permute-start(f32[2,20224]{1,0:T(2,128)S(1)} %pad_maximum_fusion.10), channel_id=1, source_target_pairs={{0,504},{4,508},{8,0},{12,4},{16,8},{20,12},{24,16},{28,20},{32,24... | collective-permute-start | bytes 485384 | tf_op jit(solution)/shard_map/ppermute | solution.py:34
  67.4 7.5 %collective-permute-start.4 = (f32[8,1,1024]{2,0,1:T(8,128)S(1)}, f32[8,1,1024]{2,0,1:T(8,128)S(1)}, u32[]{:S(2)}, u32[]{:S(2)}) collective-permute-start(f32[8,1,1024]{2,0,1:T(8,128)S(1)} %get-tuple-element.124), channel_id=1, source_target_pairs={{1,0},{2,1},{3,2},{5,4},{6,5},{7,6},{9,8},{10,9},{11,10},{13,12},{... | collective-permute-start | bytes 98312 | tf_op jit(solution)/shard_map/ppermute | solution.py:26
  68.7 6.2 %collective-permute-start.5 = (f32[8,1,1024]{2,0,1:T(8,128)S(1)}, f32[8,1,1024]{2,0,1:T(8,128)S(1)}, u32[]{:S(2)}, u32[]{:S(2)}) collective-permute-start(f32[8,1,1024]{2,0,1:T(8,128)S(1)} %get-tuple-element.125), channel_id=1, source_target_pairs={{0,1},{1,2},{2,3},{4,5},{5,6},{6,7},{8,9},{9,10},{10,11},{12,13},{... | collective-permute-start | bytes 98312 | tf_op jit(solution)/shard_map/ppermute | solution.py:25
  83.6 6.1 %collective-permute-start.6 = (f32[8,1,256]{2,0,1:T(8,128)S(1)}, f32[8,1,256]{2,0,1:T(8,128)S(1)}, u32[]{:S(2)}, u32[]{:S(2)}) collective-permute-start(f32[8,1,256]{2,0,1:T(8,128)S(1)} %get-tuple-element.138), channel_id=1, source_target_pairs={{1,0},{2,1},{3,2},{5,4},{6,5},{7,6},{9,8},{10,9},{11,10},{13,12},{... | collective-permute-start | bytes 24584 | tf_op jit(solution)/shard_map/ppermute | solution.py:26
  84.9 5.0 %collective-permute-start.7 = (f32[8,1,256]{2,0,1:T(8,128)S(1)}, f32[8,1,256]{2,0,1:T(8,128)S(1)}, u32[]{:S(2)}, u32[]{:S(2)}) collective-permute-start(f32[8,1,256]{2,0,1:T(8,128)S(1)} %get-tuple-element.139), channel_id=1, source_target_pairs={{0,1},{1,2},{2,3},{4,5},{5,6},{6,7},{8,9},{9,10},{10,11},{12,13},{... | collective-permute-start | bytes 24584 | tf_op jit(solution)/shard_map/ppermute | solution.py:25
  90.7 5.6 %collective-permute-start.8 = (f32[8,1,64]{2,0,1:T(8,128)S(1)}, f32[8,1,64]{2,0,1:T(8,128)S(1)}, u32[]{:S(2)}, u32[]{:S(2)}) collective-permute-start(f32[8,1,64]{2,0,1:T(8,128)S(1)} %get-tuple-element.150), channel_id=1, source_target_pairs={{1,0},{2,1},{3,2},{5,4},{6,5},{7,6},{9,8},{10,9},{11,10},{13,12},{... | collective-permute-start | bytes 6152 | tf_op jit(solution)/shard_map/ppermute | solution.py:26
  92.0 5.0 %collective-permute-start.9 = (f32[8,1,64]{2,0,1:T(8,128)S(1)}, f32[8,1,64]{2,0,1:T(8,128)S(1)}, u32[]{:S(2)}, u32[]{:S(2)}) collective-permute-start(f32[8,1,64]{2,0,1:T(8,128)S(1)} %get-tuple-element.151), channel_id=1, source_target_pairs={{0,1},{1,2},{2,3},{4,5},{5,6},{6,7},{8,9},{9,10},{10,11},{12,13},{... | collective-permute-start | bytes 6152 | tf_op jit(solution)/shard_map/ppermute | solution.py:25
  97.1 5.5 %collective-permute-start.10 = (f32[8,1,64]{2,0,1:T(8,128)S(1)}, f32[8,1,64]{2,0,1:T(8,128)S(1)}, u32[]{:S(2)}, u32[]{:S(2)}) collective-permute-start(f32[8,1,64]{2,0,1:T(8,128)S(1)} %get-tuple-element.148), channel_id=1, source_target_pairs={{1,0},{2,1},{3,2},{5,4},{6,5},{7,6},{9,8},{10,9},{11,10},{13,12},{... | collective-permute-start | bytes 6152 | tf_op jit(solution)/shard_map/ppermute | solution.py:26
  98.4 5.0 %collective-permute-start.11 = (f32[8,1,64]{2,0,1:T(8,128)S(1)}, f32[8,1,64]{2,0,1:T(8,128)S(1)}, u32[]{:S(2)}, u32[]{:S(2)}) collective-permute-start(f32[8,1,64]{2,0,1:T(8,128)S(1)} %get-tuple-element.149), channel_id=1, source_target_pairs={{0,1},{1,2},{2,3},{4,5},{5,6},{6,7},{8,9},{9,10},{10,11},{12,13},{... | collective-permute-start | bytes 6152 | tf_op jit(solution)/shard_map/ppermute | solution.py:25
  103.5 5.5 %collective-permute-start.12 = (f32[8,1,64]{2,0,1:T(8,128)S(1)}, f32[8,1,64]{2,0,1:T(8,128)S(1)}, u32[]{:S(2)}, u32[]{:S(2)}) collective-permute-start(f32[8,1,64]{2,0,1:T(8,128)S(1)} %get-tuple-element.146), channel_id=1, source_target_pairs={{1,0},{2,1},{3,2},{5,4},{6,5},{7,6},{9,8},{10,9},{11,10},{13,12},{... | collective-permute-start | bytes 6152 | tf_op jit(solution)/shard_map/ppermute | solution.py:26
  104.8 5.0 %collective-permute-start.13 = (f32[8,1,64]{2,0,1:T(8,128)S(1)}, f32[8,1,64]{2,0,1:T(8,128)S(1)}, u32[]{:S(2)}, u32[]{:S(2)}) collective-permute-start(f32[8,1,64]{2,0,1:T(8,128)S(1)} %get-tuple-element.147), channel_id=1, source_target_pairs={{0,1},{1,2},{2,3},{4,5},{5,6},{6,7},{8,9},{9,10},{10,11},{12,13},{... | collective-permute-start | bytes 6152 | tf_op jit(solution)/shard_map/ppermute | solution.py:25
  110.3 5.5 %collective-permute-start.14 = (f32[8,1,256]{2,0,1:T(8,128)S(1)}, f32[8,1,256]{2,0,1:T(8,128)S(1)}, u32[]{:S(2)}, u32[]{:S(2)}) collective-permute-start(f32[8,1,256]{2,0,1:T(8,128)S(1)} %get-tuple-element.136), channel_id=1, source_target_pairs={{1,0},{2,1},{3,2},{5,4},{6,5},{7,6},{9,8},{10,9},{11,10},{13,12},{... | collective-permute-start | bytes 24584 | tf_op jit(solution)/shard_map/ppermute | solution.py:26
  111.6 5.0 %collective-permute-start.15 = (f32[8,1,256]{2,0,1:T(8,128)S(1)}, f32[8,1,256]{2,0,1:T(8,128)S(1)}, u32[]{:S(2)}, u32[]{:S(2)}) collective-permute-start(f32[8,1,256]{2,0,1:T(8,128)S(1)} %get-tuple-element.137), channel_id=1, source_target_pairs={{0,1},{1,2},{2,3},{4,5},{5,6},{6,7},{8,9},{9,10},{10,11},{12,13},{... | collective-permute-start | bytes 24584 | tf_op jit(solution)/shard_map/ppermute | solution.py:25
  123.9 5.6 %collective-permute-start.16 = (f32[8,1,1024]{2,0,1:T(8,128)S(1)}, f32[8,1,1024]{2,0,1:T(8,128)S(1)}, u32[]{:S(2)}, u32[]{:S(2)}) collective-permute-start(f32[8,1,1024]{2,0,1:T(8,128)S(1)} %get-tuple-element.120), channel_id=1, source_target_pairs={{1,0},{2,1},{3,2},{5,4},{6,5},{7,6},{9,8},{10,9},{11,10},{13,12},{... | collective-permute-start | bytes 98312 | tf_op jit(solution)/shard_map/ppermute | solution.py:26
  125.2 5.3 %collective-permute-start.17 = (f32[8,1,1024]{2,0,1:T(8,128)S(1)}, f32[8,1,1024]{2,0,1:T(8,128)S(1)}, u32[]{:S(2)}, u32[]{:S(2)}) collective-permute-start(f32[8,1,1024]{2,0,1:T(8,128)S(1)} %get-tuple-element.121), channel_id=1, source_target_pairs={{0,1},{1,2},{2,3},{4,5},{5,6},{6,7},{8,9},{9,10},{10,11},{12,13},{... | collective-permute-start | bytes 98312 | tf_op jit(solution)/shard_map/ppermute | solution.py:25
  130.9 5.6 %collective-permute-start.18 = (f32[8,1,1024]{2,0,1:T(8,128)S(1)}, f32[8,1,1024]{2,0,1:T(8,128)S(1)}, u32[]{:S(2)}, u32[]{:S(2)}) collective-permute-start(f32[8,1,1024]{2,0,1:T(8,128)S(1)} %get-tuple-element.118), channel_id=1, source_target_pairs={{1,0},{2,1},{3,2},{5,4},{6,5},{7,6},{9,8},{10,9},{11,10},{13,12},{... | collective-permute-start | bytes 98312 | tf_op jit(solution)/shard_map/ppermute | solution.py:26
  132.2 5.3 %collective-permute-start.19 = (f32[8,1,1024]{2,0,1:T(8,128)S(1)}, f32[8,1,1024]{2,0,1:T(8,128)S(1)}, u32[]{:S(2)}, u32[]{:S(2)}) collective-permute-start(f32[8,1,1024]{2,0,1:T(8,128)S(1)} %get-tuple-element.119), channel_id=1, source_target_pairs={{0,1},{1,2},{2,3},{4,5},{5,6},{6,7},{8,9},{9,10},{10,11},{12,13},{... | collective-permute-start | bytes 98312 | tf_op jit(solution)/shard_map/ppermute | solution.py:25
  138.0 5.6 %collective-permute-start.20 = (f32[8,1,1024]{2,0,1:T(8,128)S(1)}, f32[8,1,1024]{2,0,1:T(8,128)S(1)}, u32[]{:S(2)}, u32[]{:S(2)}) collective-permute-start(f32[8,1,1024]{2,0,1:T(8,128)S(1)} %get-tuple-element.116), channel_id=1, source_target_pairs={{1,0},{2,1},{3,2},{5,4},{6,5},{7,6},{9,8},{10,9},{11,10},{13,12},{... | collective-permute-start | bytes 98312 | tf_op jit(solution)/shard_map/ppermute | solution.py:26
  139.3 5.3 %collective-permute-start.21 = (f32[8,1,1024]{2,0,1:T(8,128)S(1)}, f32[8,1,1024]{2,0,1:T(8,128)S(1)}, u32[]{:S(2)}, u32[]{:S(2)}) collective-permute-start(f32[8,1,1024]{2,0,1:T(8,128)S(1)} %get-tuple-element.117), channel_id=1, source_target_pairs={{0,1},{1,2},{2,3},{4,5},{5,6},{6,7},{8,9},{9,10},{10,11},{12,13},{... | collective-permute-start | bytes 98312 | tf_op jit(solution)/shard_map/ppermute | solution.py:25
  153.1 5.7 %collective-permute-start.22 = (f32[8,1,256]{2,0,1:T(8,128)S(1)}, f32[8,1,256]{2,0,1:T(8,128)S(1)}, u32[]{:S(2)}, u32[]{:S(2)}) collective-permute-start(f32[8,1,256]{2,0,1:T(8,128)S(1)} %get-tuple-element.134), channel_id=1, source_target_pairs={{1,0},{2,1},{3,2},{5,4},{6,5},{7,6},{9,8},{10,9},{11,10},{13,12},{... | collective-permute-start | bytes 24584 | tf_op jit(solution)/shard_map/ppermute | solution.py:26
  154.4 5.1 %collective-permute-start.23 = (f32[8,1,256]{2,0,1:T(8,128)S(1)}, f32[8,1,256]{2,0,1:T(8,128)S(1)}, u32[]{:S(2)}, u32[]{:S(2)}) collective-permute-start(f32[8,1,256]{2,0,1:T(8,128)S(1)} %get-tuple-element.135), channel_id=1, source_target_pairs={{0,1},{1,2},{2,3},{4,5},{5,6},{6,7},{8,9},{9,10},{10,11},{12,13},{... | collective-permute-start | bytes 24584 | tf_op jit(solution)/shard_map/ppermute | solution.py:25
  160.2 5.6 %collective-permute-start.24 = (f32[8,1,64]{2,0,1:T(8,128)S(1)}, f32[8,1,64]{2,0,1:T(8,128)S(1)}, u32[]{:S(2)}, u32[]{:S(2)}) collective-permute-start(f32[8,1,64]{2,0,1:T(8,128)S(1)} %get-tuple-element.144), channel_id=1, source_target_pairs={{1,0},{2,1},{3,2},{5,4},{6,5},{7,6},{9,8},{10,9},{11,10},{13,12},{... | collective-permute-start | bytes 6152 | tf_op jit(solution)/shard_map/ppermute | solution.py:26
  161.5 5.0 %collective-permute-start.25 = (f32[8,1,64]{2,0,1:T(8,128)S(1)}, f32[8,1,64]{2,0,1:T(8,128)S(1)}, u32[]{:S(2)}, u32[]{:S(2)}) collective-permute-start(f32[8,1,64]{2,0,1:T(8,128)S(1)} %get-tuple-element.145), channel_id=1, source_target_pairs={{0,1},{1,2},{2,3},{4,5},{5,6},{6,7},{8,9},{9,10},{10,11},{12,13},{... | collective-permute-start | bytes 6152 | tf_op jit(solution)/shard_map/ppermute | solution.py:25
  166.6 5.5 %collective-permute-start.26 = (f32[8,1,64]{2,0,1:T(8,128)S(1)}, f32[8,1,64]{2,0,1:T(8,128)S(1)}, u32[]{:S(2)}, u32[]{:S(2)}) collective-permute-start(f32[8,1,64]{2,0,1:T(8,128)S(1)} %get-tuple-element.142), channel_id=1, source_target_pairs={{1,0},{2,1},{3,2},{5,4},{6,5},{7,6},{9,8},{10,9},{11,10},{13,12},{... | collective-permute-start | bytes 6152 | tf_op jit(solution)/shard_map/ppermute | solution.py:26
  167.9 5.0 %collective-permute-start.27 = (f32[8,1,64]{2,0,1:T(8,128)S(1)}, f32[8,1,64]{2,0,1:T(8,128)S(1)}, u32[]{:S(2)}, u32[]{:S(2)}) collective-permute-start(f32[8,1,64]{2,0,1:T(8,128)S(1)} %get-tuple-element.143), channel_id=1, source_target_pairs={{0,1},{1,2},{2,3},{4,5},{5,6},{6,7},{8,9},{9,10},{10,11},{12,13},{... | collective-permute-start | bytes 6152 | tf_op jit(solution)/shard_map/ppermute | solution.py:25
  173.0 5.5 %collective-permute-start.28 = (f32[8,1,64]{2,0,1:T(8,128)S(1)}, f32[8,1,64]{2,0,1:T(8,128)S(1)}, u32[]{:S(2)}, u32[]{:S(2)}) collective-permute-start(f32[8,1,64]{2,0,1:T(8,128)S(1)} %get-tuple-element.140), channel_id=1, source_target_pairs={{1,0},{2,1},{3,2},{5,4},{6,5},{7,6},{9,8},{10,9},{11,10},{13,12},{... | collective-permute-start | bytes 6152 | tf_op jit(solution)/shard_map/ppermute | solution.py:26
  174.3 5.0 %collective-permute-start.29 = (f32[8,1,64]{2,0,1:T(8,128)S(1)}, f32[8,1,64]{2,0,1:T(8,128)S(1)}, u32[]{:S(2)}, u32[]{:S(2)}) collective-permute-start(f32[8,1,64]{2,0,1:T(8,128)S(1)} %get-tuple-element.141), channel_id=1, source_target_pairs={{0,1},{1,2},{2,3},{4,5},{5,6},{6,7},{8,9},{9,10},{10,11},{12,13},{... | collective-permute-start | bytes 6152 | tf_op jit(solution)/shard_map/ppermute | solution.py:25
  179.8 5.5 %collective-permute-start.30 = (f32[8,1,256]{2,0,1:T(8,128)S(1)}, f32[8,1,256]{2,0,1:T(8,128)S(1)}, u32[]{:S(2)}, u32[]{:S(2)}) collective-permute-start(f32[8,1,256]{2,0,1:T(8,128)S(1)} %get-tuple-element.132), channel_id=1, source_target_pairs={{1,0},{2,1},{3,2},{5,4},{6,5},{7,6},{9,8},{10,9},{11,10},{13,12},{... | collective-permute-start | bytes 24584 | tf_op jit(solution)/shard_map/ppermute | solution.py:26
  181.1 5.0 %collective-permute-start.31 = (f32[8,1,256]{2,0,1:T(8,128)S(1)}, f32[8,1,256]{2,0,1:T(8,128)S(1)}, u32[]{:S(2)}, u32[]{:S(2)}) collective-permute-start(f32[8,1,256]{2,0,1:T(8,128)S(1)} %get-tuple-element.133), channel_id=1, source_target_pairs={{0,1},{1,2},{2,3},{4,5},{5,6},{6,7},{8,9},{9,10},{10,11},{12,13},{... | collective-permute-start | bytes 24584 | tf_op jit(solution)/shard_map/ppermute | solution.py:25
  186.4 13.5 %copy-start = (f32[8,8,1024]{2,0,1:T(8,128)S(1)}, f32[8,8,1024]{2,0,1:T(8,128)}, u32[]{:S(2)}) copy-start(f32[8,8,1024]{2,0,1:T(8,128)} %get-tuple-element.157) | copy-start | bytes 786436
  193.4 5.6 %collective-permute-start.32 = (f32[8,1,1024]{2,0,1:T(8,128)S(1)}, f32[8,1,1024]{2,0,1:T(8,128)S(1)}, u32[]{:S(2)}, u32[]{:S(2)}) collective-permute-start(f32[8,1,1024]{2,0,1:T(8,128)S(1)} %get-tuple-element.112), channel_id=1, source_target_pairs={{1,0},{2,1},{3,2},{5,4},{6,5},{7,6},{9,8},{10,9},{11,10},{13,12},{... | collective-permute-start | bytes 98312 | tf_op jit(solution)/shard_map/ppermute | solution.py:26
  194.7 5.3 %collective-permute-start.33 = (f32[8,1,1024]{2,0,1:T(8,128)S(1)}, f32[8,1,1024]{2,0,1:T(8,128)S(1)}, u32[]{:S(2)}, u32[]{:S(2)}) collective-permute-start(f32[8,1,1024]{2,0,1:T(8,128)S(1)} %get-tuple-element.113), channel_id=1, source_target_pairs={{0,1},{1,2},{2,3},{4,5},{5,6},{6,7},{8,9},{9,10},{10,11},{12,13},{... | collective-permute-start | bytes 98312 | tf_op jit(solution)/shard_map/ppermute | solution.py:25
  218.6 21.7 %collective-permute-start.34 = (f32[2,8,1024]{2,0,1:T(2,128)S(1)}, f32[2,8,1024]{2,0,1:T(2,128)S(1)}, u32[]{:S(2)}, u32[]{:S(2)}) collective-permute-start(f32[2,8,1024]{2,0,1:T(2,128)S(1)} %convolution_add_fusion.6), channel_id=1, source_target_pairs={{0,4},{4,8},{8,12},{12,16},{16,20},{20,24},{24,28},{28,32},{32,36}... | collective-permute-start | bytes 196616 | tf_op jit(solution)/shard_map/ppermute | solution.py:34
  238.1 9.1 %collective-permute-start.35 = (f32[2,8,1024]{2,0,1:T(2,128)S(1)}, f32[2,8,1024]{2,0,1:T(2,128)S(1)}, u32[]{:S(2)}, u32[]{:S(2)}) collective-permute-start(f32[2,8,1024]{2,0,1:T(2,128)S(1)} %convolution_add_fusion.5), channel_id=1, source_target_pairs={{0,8},{4,12},{8,16},{12,20},{16,24},{20,28},{24,32},{28,36},{32,40... | collective-permute-start | bytes 196616 | tf_op jit(solution)/shard_map/ppermute | solution.py:34
where the time goes:
time: 252 us; the launch traced here: 248 us
  starting transfers between devices  127 us (50%)
  local copies, waits for them, and re-layouts  71.3 us (28%)
  other arithmetic  19.6 us (8%)
  waiting for transfers between devices  19.5 us (8%)
  matrix products  9.16 us (4%)
    ppermute x16, starting transfers between devices, extended_2(): before = lax.ppermute(last, axis, up)  68.7 us
    ppermute x4, starting transfers between devices, passed_along(): return lax.ppermute(value, axis, pairs)  37.5 us
    gather x64, local copies, waits for them, and re-layouts  33.8 us
    ppermute x16, starting transfers between devices, extended_2(): after = lax.ppermute(initial, axis, down)  20.7 us
    reduce_sum x6, other arithmetic, coarsen(): grouped.mean(axis=(2, 4, 6))  14.8 us
    ppermute x16, waiting for transfers between devices, extended_2(): before = lax.ppermute(last, axis, up)  10.5 us
    reshape x1, local copies, waits for them, and re-layouts, coarsen(): values.reshape(slot_count, layer_count // 2, 2, half_edge, 2, half_edge, 2)  9.81 us
    broadcast_in_dim x8, local copies, waits for them, and re-layouts, refine(): jnp.broadcast_to(values.reshape(slot_count, layer_count, 1, half_edge, 1,...  9.2 us
  transfers between devices with their start and end apart: 36, of which 16 were waited for; matrix products, arithmetic and copies ran while one was open for 4% of the time, Pallas kernels for 0%

commit v1 on v0

v1 whole, which is shorter than its diff:
```python
import functools

import jax
import jax.numpy as jnp
from jax import lax
from jax.experimental import pallas as pl
from jax.experimental.pallas import tpu as pltpu
from jax.sharding import PartitionSpec as P

B = 32
PMAX = 4
SMAX = 8
CYCLES = 2
SWEEPS = 4
FOURPI = 4.0 * 3.141592653589793
OMEGA = 0.8

SECOND = ((1, 4, 4, 5, 4, 5, 4, 5), (2, 3, 2, 3, 3, 6, 6, 7))
PLACE = ((1, 4, 4, 5, 4, 5, 4, 5), (2, 3, 2, 3, 3, 4, 4, 5))
SLOTS = 8
FRONT = 2
PADDED = 13
ROWS = 64
LANES = 128


def as_rows(value):
    count = value.shape[0]
    return value.reshape(count, 8, 8, LANES).transpose(0, 2, 1, 3).reshape(count, ROWS, LANES)


def from_rows(value):
    count = value.shape[0]
    return value.reshape(count, 8, 8, LANES).transpose(0, 2, 1, 3).reshape(count, 8, 8 * LANES)


def lane_of(shape):
    return lax.broadcasted_iota(jnp.int32, shape, len(shape) - 1)


def fill_padded(pad, place, source, index):
    for block in range(8):
        pad[place, FRONT + block] = source[index, 8 * block : 8 * block + 8, :]


def clear_margins(pad, count):
    nothing = jnp.zeros((8, LANES), jnp.float32)
    for place in range(count):
        for block in (0, 1, 10, 11, 12):
            pad[place, block] = nothing


def shifted(pad, place, delta):
    moved = delta + SMAX
    first = moved >> 2
    part = moved & 3
    turn = (LANES - 32 * part) & (LANES - 1)
    keep = lane_of((8, LANES)) < LANES - 32 * part
    rolled = [pltpu.roll(pad[place, first + block], turn, 1) for block in range(9)]
    return [jnp.where(keep, rolled[block], rolled[block + 1]) for block in range(8)]


def gather_fields(core, own_ref, swap_ref, next_ref, pad):
    for index in range(2):
        fill_padded(pad, 2 * core + index, own_ref, index)
        fill_padded(pad, 2 * (1 - core) + index, swap_ref, index)
        fill_padded(pad, 4 + index, next_ref, index)
    clear_margins(pad, 6)


def pre_kernel(table_ref, own_ref, eps_ref, swap_ref, next_ref, out_ref, pad):
    core = table_ref[2 * SLOTS]
    gather_fields(core, own_ref, swap_ref, next_ref, pad)
    for slot in range(SLOTS):
        moved = shifted(pad, table_ref[SLOTS + slot], table_ref[slot])
        for block in range(8):
            first = pad[slot // 2, FRONT + block]
            out_ref[slot // 2, slot % 2, 8 * block : 8 * block + 8, :] = FOURPI * (
                first * moved[block]
            )
    for index in range(2):
        out_ref[2 * core + index, 2] = eps_ref[index]
        out_ref[2 * (1 - core) + index, 2] = swap_ref[2 + index]


def post_kernel(
    table_ref, own_ref, swap_ref, next_ref, pot_ref, own_out, swap_out, next_out, pad, back, acc
):
    core = table_ref[2 * SLOTS]
    gather_fields(core, own_ref, swap_ref, next_ref, pad)
    clear_margins(back, 2)
    nothing = jnp.zeros((ROWS, LANES), jnp.float32)
    for place in range(6):
        acc[place] = nothing
    for slot in range(SLOTS):
        delta = table_ref[slot]
        place = table_ref[SLOTS + slot]
        live = table_ref[2 * SLOTS + 1 + slot] > 0
        moved = shifted(pad, place, delta)
        for block in range(8):
            rows = slice(8 * block, 8 * block + 8)
            value = jnp.where(live, pot_ref[slot // 2, slot % 2, rows, :], 0.0)
            acc[slot // 2, rows, :] = acc[slot // 2, rows, :] - value * moved[block]
            back[slot % 2, FRONT + block] = value * pad[slot // 2, FRONT + block]
        returned = shifted(back, slot % 2, -delta)
        for block in range(8):
            rows = slice(8 * block, 8 * block + 8)
            acc[place, rows, :] = acc[place, rows, :] - returned[block]
    for index in range(2):
        own_out[index] = acc[2 * core + index]
        swap_out[index] = acc[2 * (1 - core) + index]
        next_out[index] = acc[4 + index]


def roll(value, steps, axis):
    size = value.shape[axis]
    return pltpu.roll(value, steps % size, axis)


def exchange_groups(parts):
    lane = lane_of((8, LANES))
    low = lane < 64
    even = (lane & 32) == 0
    halves = [None] * 4
    for index in range(2):
        above, below = parts[index], parts[index + 2]
        crossed = roll(jnp.where(low, below, above), 64, 1)
        halves[index] = jnp.where(low, above, crossed)
        halves[index + 2] = jnp.where(low, crossed, below)
    result = [None] * 4
    for index in (0, 2):
        left, right = halves[index], halves[index + 1]
        result[index] = jnp.where(even, left, roll(right, 32, 1))
        result[index + 1] = jnp.where(even, roll(left, -32, 1), right)
    return result


class Level:
    def __init__(self, depth):
        self.depth = depth
        self.zs = 8 >> depth
        self.ys = 4 >> depth
        self.step = 1 << depth
        lane = lane_of((8, LANES))
        sub = lax.broadcasted_iota(jnp.int32, (8, LANES), 0)
        column = lane & 31
        self.inside = (
            lane < 96,
            lane >= 32,
            sub < 7,
            sub > 0,
            column < 32 - self.step,
            column >= self.step,
        )

    def neighbours(self, get, q, r):
        zs, ys = self.zs, self.ys
        return (
            get(q + 1, r) if q < zs - 1 else roll(get(0, r), -32, 1),
            get(q - 1, r) if q > 0 else roll(get(zs - 1, r), 32, 1),
            get(q, r + 1) if r < ys - 1 else roll(get(q, 0), -1, 0),
            get(q, r - 1) if r > 0 else roll(get(q, ys - 1), 1, 0),
            roll(get(q, r), -self.step, 1),
            roll(get(q, r), self.step, 1),
        )

    def edges(self, q, r):
        return (
            self.inside[0] if q == self.zs - 1 else None,
            self.inside[1] if q == 0 else None,
            self.inside[2] if r == self.ys - 1 else None,
            self.inside[3] if r == 0 else None,
            self.inside[4],
            self.inside[5],
        )

    def coefficients(self, get, q, r):
        centre = get(q, r)
        edges = self.edges(q, r)
        around = [
            value if edge is None else jnp.where(edge, value, 0.0)
            for value, edge in zip(self.neighbours(get, q, r), edges)
        ]
        total = 6.0 * centre + sum(around[1:], around[0])
        scale = OMEGA / total
        couplings = []
        for value, edge in zip(around, edges):
            coupling = (centre + value) * scale
            couplings.append(coupling if edge is None else jnp.where(edge, coupling, 0.0))
        return couplings, total, scale

    def change(self, get, couplings, source, q, r):
        around = self.neighbours(get, q, r)
        terms = [c * v for c, v in zip(couplings, around)]
        pairs = (terms[0] + terms[1]) + (terms[2] + terms[3]) + (terms[4] + terms[5])
        return (source - OMEGA * get(q, r)) + pairs

    def pair_sum(self, value):
        even = (lane_of((8, LANES)) & self.step) == 0
        return value + jnp.where(even, roll(value, -self.step, 1), roll(value, self.step, 1))

    def block_sums(self, get):
        sums = {}
        for q in range(0, self.zs, 2):
            for r in range(0, self.ys, 2):
                four = (get(q, r) + get(q, r + 1)) + (get(q + 1, r) + get(q + 1, r + 1))
                sums[q // 2, r // 2] = self.pair_sum(four)
        return sums

    def cells(self):
        return [(q, r) for q in range(self.zs) for r in range(self.ys)]


def solve_kernel(in_ref, out_ref, eps, couple, total, source, first, second):
    levels = [Level(depth) for depth in range(3)]
    fine, half, quarter = levels

    def at(ref, *lead):
        return lambda q, r: ref[(*lead, q * 4 + r)]

    for q in range(8):
        for field in range(3):
            parts = [in_ref[part, field, pl.ds(q, 8, stride=8), :] for part in range(4)]
            turned = exchange_groups(parts)
            for r in range(4):
                if field == 2:
                    eps[q * 4 + r] = turned[r]
                else:
                    source[field, q * 4 + r] = turned[r]

    get_eps = at(eps)
    for q, r in fine.cells():
        couplings, summed, scale = fine.coefficients(get_eps, q, r)
        for side in range(6):
            couple[side, q * 4 + r] = couplings[side]
        total[q * 4 + r] = summed
        for slot in range(2):
            source[slot, q * 4 + r] = (2.0 * scale) * source[slot, q * 4 + r]

    def coarse_data(level, eps_sums):
        eps_level = {key: 0.125 * value for key, value in eps_sums.items()}
        get = lambda q, r: eps_level[q, r]
        data = {key: level.coefficients(get, *key) for key in level.cells()}
        return get, data

    get_half, half_data = coarse_data(half, fine.block_sums(get_eps))
    _, quarter_data = coarse_data(quarter, half.block_sums(get_half))

    def smooth(level, data, values, rhs):
        get = lambda q, r: values[q, r]
        return {
            key: level.change(get, data[key][0], rhs[key], *key) for key in level.cells()
        }

    def added(values, changes):
        return {key: values[key] + changes[key] for key in values}

    def restricted(level, data, changes, below, below_data):
        weighted = lambda q, r: data[q, r][1] * changes[q, r]
        sums = level.block_sums(weighted)
        return {key: (0.625 * below_data[key][2]) * sums[key] for key in below.cells()}

    def correction(rhs_half):
        values = rhs_half
        changes = smooth(half, half_data, values, rhs_half)
        rhs_quarter = restricted(half, half_data, changes, quarter, quarter_data)
        lowest = rhs_quarter
        for _ in range(SWEEPS - 1):
            lowest = added(lowest, smooth(quarter, quarter_data, lowest, rhs_quarter))
        values = {(q, r): values[q, r] + lowest[q // 2, r // 2] for q, r in half.cells()}
        return added(values, smooth(half, half_data, values, rhs_half))

    def fine_change(ref, slot, q, r):
        couplings = [couple[side, q * 4 + r] for side in range(6)]
        return fine.change(at(ref, slot), couplings, source[slot, q * 4 + r], q, r)

    def coarse_rhs(ref):
        result = [{}, {}]
        for q in range(0, 8, 2):
            for r in range(0, 4, 2):
                for slot in range(2):
                    four = None
                    for qq, rr in ((q, r), (q, r + 1), (q + 1, r), (q + 1, r + 1)):
                        term = total[qq * 4 + rr] * fine_change(ref, slot, qq, rr)
                        four = term if four is None else four + term
                    key = (q // 2, r // 2)
                    result[slot][key] = (0.625 * half_data[key][2]) * fine.pair_sum(four)
        return result

    def relax(ref, target):
        for q, r in fine.cells():
            for slot in range(2):
                target(slot, q, r, ref[slot, q * 4 + r] + fine_change(ref, slot, q, r))

    def into(ref):
        def put(slot, q, r, value):
            ref[slot, q * 4 + r] = value

        return put

    def corrected(ref, target):
        rhs = coarse_rhs(ref)
        extra = [correction(rhs[slot]) for slot in range(2)]
        for q, r in fine.cells():
            for slot in range(2):
                target[slot, q * 4 + r] = ref[slot, q * 4 + r] + extra[slot][q // 2, r // 2]

    corrected(source, first)
    for _ in range(CYCLES - 1):
        relax(first, into(second))
        relax(second, into(first))
        corrected(first, first)
    relax(first, into(second))
    for q in range(8):
        for slot in range(2):
            turned = exchange_groups([second[slot, q * 4 + r] for r in range(4)])
            for part in range(4):
                out_ref[part, slot, pl.ds(q, 8, stride=8), :] = turned[part]


def near(value):
    return pltpu.with_memory_space_constraint(value, pltpu.VMEM)


def slot_table(owner, pair_offsets, pair_counts, box_shift):
    core = owner % 2
    base = 2 * (owner - core)
    first = jnp.repeat(jnp.arange(PMAX, dtype=jnp.int32), 2)
    second = jnp.where(core == 0, jnp.array(SECOND[0], jnp.int32), jnp.array(SECOND[1], jnp.int32))
    place = jnp.where(core == 0, jnp.array(PLACE[0], jnp.int32), jnp.array(PLACE[1], jnp.int32))
    counts = lax.dynamic_slice(pair_counts, (base,), (4,))
    offsets = lax.dynamic_slice(pair_offsets, (base, 0), (4, PMAX))
    looped = jnp.concatenate([box_shift, box_shift[:4]])
    shifts = lax.dynamic_slice(looped, (base,), (8,))
    named = jnp.arange(8, dtype=jnp.int32)[None, :] == second[:, None]
    delta = jnp.repeat(shifts[:4], 2) - jnp.sum(jnp.where(named, shifts[None, :], 0), axis=1)
    listed = jnp.arange(PMAX, dtype=jnp.int32)[None, :] < jnp.repeat(counts, 2)[:, None]
    wanted = jnp.repeat(offsets, 2, axis=0) + 1 == (second - first)[:, None]
    live = jnp.any(listed & wanted, axis=1).astype(jnp.int32)
    return jnp.concatenate([delta, place, core[None].astype(jnp.int32), live])


def shards(orbitals, dielectric, pair_offsets, pair_counts, box_shift):
    owner = lax.axis_index("orb")
    owners = lax.axis_size("orb")
    swapped = [(source, source ^ 1) for source in range(owners)]
    back_chip = [(source, (source - 2) % owners) for source in range(owners)]
    next_chip = [(source, (source + 2) % owners) for source in range(owners)]

    own = as_rows(orbitals)
    eps = as_rows(dielectric)
    beyond = lax.ppermute(own, "orb", back_chip)
    across = lax.ppermute(jnp.concatenate([own, eps]), "orb", swapped)
    table = slot_table(owner, pair_offsets, pair_counts, box_shift)

    smem = pl.BlockSpec(memory_space=pltpu.SMEM)
    vmem = pl.BlockSpec(memory_space=pltpu.VMEM)
    pad_scratch = pltpu.VMEM((6, PADDED, 8, LANES), jnp.float32)
    requests = pl.pallas_call(
        pre_kernel,
        out_shape=pltpu.VMEM((4, 3, ROWS, LANES), jnp.float32),
        in_specs=[smem, vmem, vmem, vmem, vmem],
        out_specs=vmem,
        scratch_shapes=[pad_scratch],
        name="pair_sources",
    )(table, near(own), near(eps), near(across), near(beyond))
    arrived = lax.all_to_all(requests, "grid", 0, 0)
    cells = (32, 8, LANES)
    potentials = pl.pallas_call(
        solve_kernel,
        out_shape=pltpu.VMEM((4, 2, ROWS, LANES), jnp.float32),
        in_specs=[vmem],
        out_specs=vmem,
        scratch_shapes=[
            pltpu.VMEM(cells, jnp.float32),
            pltpu.VMEM((6, *cells), jnp.float32),
            pltpu.VMEM(cells, jnp.float32),
            pltpu.VMEM((2, *cells), jnp.float32),
            pltpu.VMEM((2, *cells), jnp.float32),
            pltpu.VMEM((2, *cells), jnp.float32),
        ],
        name="pair_solve",
    )(near(arrived))
    returned = lax.all_to_all(potentials, "grid", 0, 0)
    two = pltpu.VMEM((2, ROWS, LANES), jnp.float32)
    mine, theirs, later = pl.pallas_call(
        post_kernel,
        out_shape=(two, two, two),
        in_specs=[smem, vmem, vmem, vmem, vmem],
        out_specs=(vmem, vmem, vmem),
        scratch_shapes=[
            pad_scratch,
            pltpu.VMEM((2, PADDED, 8, LANES), jnp.float32),
            pltpu.VMEM((6, ROWS, LANES), jnp.float32),
        ],
        name="pair_actions",
    )(table, near(own), near(across), near(beyond), near(returned))
    from_chip = lax.ppermute(theirs, "orb", swapped)
    from_before = lax.ppermute(later, "orb", next_chip)
    return from_rows(mine + from_chip + from_before)


def solution(mesh):
    placed = (P("orb", "grid", None), P("orb", "grid", None), P(), P(), P())
    return jax.shard_map(
        shards, mesh=mesh, in_specs=placed, out_specs=P("orb", "grid", None), check_vma=False
    )
```

time: 252 us -> 60.7 us (0.24); the launches traced: 248 us -> 60.3 us
  starting transfers between devices: 127 us -> 23.5 us
  local copies, waits for them, and re-layouts: 71.3 us -> 0.9 us
  blocking collectives: 0 us -> 19.6 us
  other arithmetic: 19.6 us -> 2.66 us
  waiting for transfers between devices: 19.5 us -> 6.92 us
  matrix products: 9.16 us -> 0 us
  Pallas kernels: 0 us -> 6.49 us
    ppermute x36 -> x4, starting transfers between devices: 127 us -> 23.5 us  [the longest x1 14.4 us: shards(): beyond = lax.ppermute(own, 'orb', back_chip)]
    gather x64 -> x0, local copies, waits for them, and re-layouts: 33.8 us -> none
    all_to_all x0 -> x2, blocking collectives: none -> 19.6 us  [the longest x1 11.7 us: shards(): arrived = lax.all_to_all(requests, 'grid', 0, 0)]
    reshape x8 -> x2, local copies, waits for them, and re-layouts: 15.9 us -> 0.17 us  [the longest x1 0.09 us: slot_table(): first = jnp.repeat(jnp.arange(PMAX, dtype=jnp.int32), 2)]
    reduce_sum x8 -> x1, other arithmetic: 15.9 us -> 0.18 us  [slot_table(): jnp.sum(jnp.where(named, shifts[None, :], 0), axis=1)]
    ppermute x36 -> x4, waiting for transfers between devices: 19.5 us -> 6.92 us  [the longest x1 6.91 us: shards(): from_before = lax.ppermute(later, 'orb', next_chip)]
    broadcast_in_dim x10 -> x2, local copies, waits for them, and re-layouts: 9.32 us -> 0.07 us  [the longest x1 0.07 us: slot_table(): jnp.repeat(shifts[:4], 2)]
    dot_general x21 -> x0, matrix products: 9.16 us -> none  [the longest x12 5.42 us: shards(): jnp.einsum('sa,azf->szf', first_hot, portion, precision=HIGHEST)]
  transfers between devices with their start and end apart: 36 -> 4, of which waited for: 16 -> 1; matrix products, arithmetic and copies ran while one was open for 4% -> 5% of each run, Pallas kernels for 0% -> 0%
where the time goes in v1:
time: 60.7 us; the launch traced here: 60.3 us
  starting transfers between devices  23.5 us (39%)
  blocking collectives  19.6 us (32%)
  waiting for transfers between devices  6.92 us (11%)
  Pallas kernels  6.49 us (11%)
  other arithmetic  2.66 us (4%)
  local copies, waits for them, and re-layouts  0.9 us (1%)
    ppermute x1, starting transfers between devices, shards(): beyond = lax.ppermute(own, 'orb', back_chip)  14.4 us
    all_to_all x1, blocking collectives, shards(): arrived = lax.all_to_all(requests, 'grid', 0, 0)  11.7 us
    all_to_all x1, blocking collectives, shards(): returned = lax.all_to_all(potentials, 'grid', 0, 0)  7.92 us
    ppermute x1, waiting for transfers between devices, shards(): from_before = lax.ppermute(later, 'orb', next_chip)  6.91 us
    pallas_call x1, Pallas kernels, shards(): pl.pallas_call(solve_kernel, out_shape=pltpu.VMEM((4, 2, ROWS, LANES), jn...  4.72 us
    ppermute x1, starting transfers between devices, shards(): from_chip = lax.ppermute(theirs, 'orb', swapped)  4.21 us
    ppermute x1, starting transfers between devices, shards(): across = lax.ppermute(jnp.concatenate([own, eps]), 'orb', swapped)  3 us
    ppermute x1, starting transfers between devices, shards(): from_before = lax.ppermute(later, 'orb', next_chip)  1.92 us
  transfers between devices with their start and end apart: 4, of which 1 were waited for; matrix products, arithmetic and copies ran while one was open for 5% of the time, Pallas kernels for 0%

profile of v1, /device:TPU:1, one launch (start us, length us, event | category | flops | bytes accessed | tf_op | source)
XLA Modules:
  0.0 60.3 jit_solution(13873627696060243161)
XLA Ops:
  0.0 14.4 %collective-permute-start.1 = (f32[2,64,128]{2,1,0:T(8,128)}, f32[2,64,128]{2,1,0:T(8,128)S(1)}, u32[]{:S(2)}, u32[]{:S(2)}) collective-permute-start(f32[2,64,128]{2,1,0:T(8,128)} %bitcast.18), channel_id=1, source_target_pairs={{0,504},{4,508},{8,0},{12,4},{16,8},{20,12},{24,16},{28,20},{32,24... | collective-permute-start | bytes 196616 | tf_op jit(solution)/shard_map/ppermute | solution.py:352
  14.4 0.0 copy-start.2
  14.4 0.0 slice-start
  14.4 0.0 copy-start.7
  14.4 0.0 copy-start.3
  14.4 0.0 copy-start.4
  14.4 0.0 copy-start.5
  14.5 0.0 copy-start.6
  14.5 0.0 copy-start.1
  14.5 0.9 %pad_maximum_fusion = f32[4,64,128]{2,1,0:T(8,128)S(1)} fusion(f32[2,64,128]{2,1,0:T(8,128)} %bitcast.22, f32[2,64,128]{2,1,0:T(8,128)} %bitcast.19), kind=kLoop, calls=%fused_computation | loop fusion | flops 32768 | bytes 262144 | tf_op jit(solution)/shard_map/concatenate | solution.py:353
  15.4 0.0 copy-start
  15.4 3.0 %collective-permute-start = (f32[4,64,128]{2,1,0:T(8,128)S(1)}, f32[4,64,128]{2,1,0:T(8,128)S(1)}, u32[]{:S(2)}, u32[]{:S(2)}) collective-permute-start(f32[4,64,128]{2,1,0:T(8,128)S(1)} %pad_maximum_fusion), channel_id=1, source_target_pairs={{0,4},{4,0},{8,12},{12,8},{16,20},{20,16},{24,28},{28,24},{32,36},... | collective-permute-start | bytes 393224 | tf_op jit(solution)/shard_map/ppermute | solution.py:353
  18.4 0.0 copy-done.2
  18.5 0.0 slice-done
  18.5 0.0 copy-done.7
  18.5 0.1 dynamic_slice.10
  18.6 0.0 copy-done.3
  18.6 0.1 dynamic-slice_add_fusion
  18.7 0.1 copy.12
  18.8 0.1 reshape.46
  18.8 0.0 copy-done.4
  18.8 0.0 copy-done.5
  18.8 0.0 copy-done.6
  18.9 0.1 eq.34
  18.9 0.1 copy.13
  19.0 0.1 dynamic_slice.9
  19.1 0.2 fusion.1
  19.3 0.2 select_reduce_fusion
  19.5 0.1 broadcast_in_dim.30
  19.6 0.1 reshape.45
  19.6 0.1 copy.14
  19.7 0.1 reshape.53
  19.8 0.6 %pad_add_fusion.1.table_ref = s32[25]{0:T(128)} fusion(s32[8]{0:T(128)S(1)} %reshape.53, s32[1]{0:T(128)} %bitcast, s32[8]{0:T(128)S(1)} %get-tuple-element.13, s32[8]{0:T(128)S(1)} %sub.10), kind=kLoop, calls=%fused_computation.11 | loop fusion | flops 75 | bytes 200 | tf_op jit(solution)/shard_map/concatenate | solution.py:340
  20.4 0.0 collective-permute-done.1.next_ref
  20.5 0.0 collective-permute-done.swap_ref
  20.5 0.0 copy-done.1
  20.5 0.0 copy-done
  20.5 0.8 %pair_sources.1 = f32[4,3,64,128]{3,2,1,0:T(8,128)S(1)} custom-call(s32[25]{0:T(128)} %pad_add_fusion.1.table_ref, f32[2,64,128]{2,1,0:T(8,128)S(1)} %bitcast.20, f32[2,64,128]{2,1,0:T(8,128)S(1)} %bitcast.23, f32[4,64,128]{2,1,0:T(8,128)S(1)} %collective-permute-done.swap_ref, f32[2,64,128]{2,1,0:T(8,128)S(1)} %collective-permute-done.1.next_ref), custom_call_target="tpu_custom_call" | custom-call | tf_op jit(solution)/shard_map/pair_sources/pallas_call | solution.py:359
  21.3 11.7 %all_to_all.10.in_ref = f32[4,3,64,128]{3,2,1,0:T(8,128)S(1)} all-to-all(f32[4,3,64,128]{3,2,1,0:T(8,128)S(1)} %pair_sources.1), channel_id=1, replica_groups=mesh['orb'=128,'grid'=4] {'grid'}, dimensions={0} | all-to-all | bytes 786432 | tf_op jit(solution)/shard_map/all_to_all | solution.py:367
  33.0 4.7 %pair_solve.1 = f32[4,2,64,128]{3,2,1,0:T(8,128)S(1)} custom-call(f32[4,3,64,128]{3,2,1,0:T(8,128)S(1)} %all_to_all.10.in_ref), custom_call_target="tpu_custom_call" | custom-call | tf_op jit(solution)/shard_map/pair_solve/pallas_call | solution.py:369
  37.7 7.9 %all_to_all.11.pot_ref = f32[4,2,64,128]{3,2,1,0:T(8,128)S(1)} all-to-all(f32[4,2,64,128]{3,2,1,0:T(8,128)S(1)} %pair_solve.1), channel_id=1, replica_groups=mesh['orb'=128,'grid'=4] {'grid'}, dimensions={0} | all-to-all | bytes 524288 | tf_op jit(solution)/shard_map/all_to_all | solution.py:384
  45.7 0.9 %pair_actions.1 = (f32[2,64,128]{2,1,0:T(8,128)S(1)}, f32[2,64,128]{2,1,0:T(8,128)S(1)}, f32[2,64,128]{2,1,0:T(8,128)S(1)}) custom-call(s32[25]{0:T(128)} %pad_add_fusion.1.table_ref, f32[2,64,128]{2,1,0:T(8,128)S(1)} %bitcast.21, f32[4,64,128]{2,1,0:T(8,128)S(1)} %collective-permute-done.swap_ref, f32[2,64,128]{2,1,0:T(8,128)S(1)} %collective-permute-done.1.next_ref, ...), custom_call_target="tpu_custom_call" | custom-call | tf_op jit(solution)/shard_map/pair_actions/pallas_call | solution.py:386
  46.6 4.2 %collective-permute-start.2 = (f32[2,64,128]{2,1,0:T(8,128)S(1)}, f32[2,64,128]{2,1,0:T(8,128)S(1)}, u32[]{:S(2)}, u32[]{:S(2)}) collective-permute-start(f32[2,64,128]{2,1,0:T(8,128)S(1)} %get-tuple-element.9), channel_id=1, source_target_pairs={{0,4},{4,0},{8,12},{12,8},{16,20},{20,16},{24,28},{28,24},{32,36},... | collective-permute-start | bytes 196616 | tf_op jit(solution)/shard_map/ppermute | solution.py:398
  50.8 1.9 %collective-permute-start.3 = (f32[2,64,128]{2,1,0:T(8,128)S(1)}, f32[2,64,128]{2,1,0:T(8,128)S(1)}, u32[]{:S(2)}, u32[]{:S(2)}) collective-permute-start(f32[2,64,128]{2,1,0:T(8,128)S(1)} %get-tuple-element.10), channel_id=1, source_target_pairs={{0,8},{4,12},{8,16},{12,20},{16,24},{20,28},{24,32},{28,36},{32,40... | collective-permute-start | bytes 196616 | tf_op jit(solution)/shard_map/ppermute | solution.py:399
  52.7 0.0 collective-permute-done.2
  52.8 6.9 %collective-permute-done.3 = f32[2,64,128]{2,1,0:T(8,128)S(1)} collective-permute-done((f32[2,64,128]{2,1,0:T(8,128)S(1)}, f32[2,64,128]{2,1,0:T(8,128)S(1)}, u32[]{:S(2)}, u32[]{:S(2)}) %collective-permute-start.3) | collective-permute-done | bytes 65568 | tf_op jit(solution)/shard_map/ppermute | solution.py:399
  59.7 0.6 %add_bitcast_fusion = f32[2,8,1024]{2,1,0:T(8,128)} fusion(f32[2,64,128]{2,1,0:T(8,128)S(1)} %collective-permute-done.3, f32[2,64,128]{2,1,0:T(8,128)S(1)} %get-tuple-element.8, f32[2,64,128]{2,1,0:T(8,128)S(1)} %collective-permute-done.2), kind=kLoop, calls=%fused_computation.1 | loop fusion | flops 32768 | bytes 262144 | tf_op jit(solution)/shard_map/reshape | solution.py:34
  (5 shorter events, 0.0 us)
Async XLA Ops:
  0.0 20.5 %collective-permute-start.1 = (f32[2,64,128]{2,1,0:T(8,128)}, f32[2,64,128]{2,1,0:T(8,128)S(1)}, u32[]{:S(2)}, u32[]{:S(2)}) collective-permute-start(f32[2,64,128]{2,1,0:T(8,128)} %bitcast.18), channel_id=1, source_target_pairs={{0,504},{4,508},{8,0},{12,4},{16,8},{20,12},{24,16},{28,20},{32,24... | collective-permute-start | bytes 196616 | tf_op jit(solution)/shard_map/ppermute | solution.py:352
  14.4 4.1 %copy-start.2 = (s32[256]{0:T(256)S(1)}, s32[256]{0:T(256)}, u32[]{:S(2)}) copy-start(s32[256]{0:T(256)} %param.13) | copy-start | bytes 3076
  14.4 4.1 %slice-start = ((s32[256]{0:T(256)}), s32[4]{0:T(128)S(1)}, s32[]{:S(2)}) async-start(s32[256]{0:T(256)} %param.13), calls=%async_computation.2 | async-start | bytes 1024 | tf_op jit(solution)/shard_map/slice | solution.py:333
  14.4 4.1 %copy-start.7 = (s32[256]{0:T(256)S(1)}, s32[256]{0:T(256)}, u32[]{:S(2)}) copy-start(s32[256]{0:T(256)} %param.12) | copy-start | bytes 3076
  14.4 4.2 %copy-start.3 = (s32[256,4]{0,1:T(4,128)S(1)}, s32[256,4]{0,1:T(4,128)}, u32[]{:S(2)}) copy-start(s32[256,4]{0,1:T(4,128)} %param.11) | copy-start | bytes 12292
  14.4 4.4 %copy-start.4 = (s32[8]{0:T(128)S(1)}, s32[8]{0:T(128)}, u32[]{:S(2)}) copy-start(s32[8]{0:T(128)} %constant.35.clone) | copy-start | bytes 100
  14.4 4.4 %copy-start.5 = (s32[8]{0:T(128)S(1)}, s32[8]{0:T(128)}, u32[]{:S(2)}) copy-start(s32[8]{0:T(128)} %constant.34.clone) | copy-start | bytes 100
  14.5 4.4 %copy-start.6 = (s32[8]{0:T(128)S(1)}, s32[8]{0:T(128)}, u32[]{:S(2)}) copy-start(s32[8]{0:T(128)} %constant.33.clone) | copy-start | bytes 100
  14.5 6.0 %copy-start.1 = (f32[2,8,1024]{2,1,0:T(8,128)S(1)}, f32[2,8,1024]{2,1,0:T(8,128)}, u32[]{:S(2)}) copy-start(f32[2,8,1024]{2,1,0:T(8,128)} %param.10) | copy-start | bytes 196612
  15.4 5.1 %copy-start = (f32[2,8,1024]{2,1,0:T(8,128)S(1)}, f32[2,8,1024]{2,1,0:T(8,128)}, u32[]{:S(2)}) copy-start(f32[2,8,1024]{2,1,0:T(8,128)} %param.9) | copy-start | bytes 196612
  15.4 5.0 %collective-permute-start = (f32[4,64,128]{2,1,0:T(8,128)S(1)}, f32[4,64,128]{2,1,0:T(8,128)S(1)}, u32[]{:S(2)}, u32[]{:S(2)}) collective-permute-start(f32[4,64,128]{2,1,0:T(8,128)S(1)} %pad_maximum_fusion), channel_id=1, source_target_pairs={{0,4},{4,0},{8,12},{12,8},{16,20},{20,16},{24,28},{28,24},{32,36},... | collective-permute-start | bytes 393224 | tf_op jit(solution)/shard_map/ppermute | solution.py:353
  46.6 6.1 %collective-permute-start.2 = (f32[2,64,128]{2,1,0:T(8,128)S(1)}, f32[2,64,128]{2,1,0:T(8,128)S(1)}, u32[]{:S(2)}, u32[]{:S(2)}) collective-permute-start(f32[2,64,128]{2,1,0:T(8,128)S(1)} %get-tuple-element.9), channel_id=1, source_target_pairs={{0,4},{4,0},{8,12},{12,8},{16,20},{20,16},{24,28},{28,24},{32,36},... | collective-permute-start | bytes 196616 | tf_op jit(solution)/shard_map/ppermute | solution.py:398
  50.8 8.8 %collective-permute-start.3 = (f32[2,64,128]{2,1,0:T(8,128)S(1)}, f32[2,64,128]{2,1,0:T(8,128)S(1)}, u32[]{:S(2)}, u32[]{:S(2)}) collective-permute-start(f32[2,64,128]{2,1,0:T(8,128)S(1)} %get-tuple-element.10), channel_id=1, source_target_pairs={{0,8},{4,12},{8,16},{12,20},{16,24},{20,28},{24,32},{28,36},{32,40... | collective-permute-start | bytes 196616 | tf_op jit(solution)/shard_map/ppermute | solution.py:399

commit v2 on v1

v2 whole, which is shorter than its diff:
```python
import jax
import jax.numpy as jnp
from jax import lax
from jax.experimental import pallas as pl
from jax.experimental.pallas import tpu as pltpu
from jax.sharding import PartitionSpec as P

PMAX = 4
SMAX = 8
CYCLES = 2
SWEEPS = 4
FOURPI = 4.0 * 3.141592653589793
OMEGA = 0.8

SECOND = ((1, 4, 4, 5, 4, 5, 4, 5), (2, 3, 2, 3, 3, 6, 6, 7))
PLACE = ((1, 4, 4, 5, 4, 5, 4, 5), (2, 3, 2, 3, 3, 4, 4, 5))
SLOTS = 8
FRONT = 2
PADDED = 13
ROWS = 64
LANES = 128


def as_rows(value):
    count = value.shape[0]
    return value.reshape(count, 8, 8, LANES).transpose(0, 2, 1, 3).reshape(count, ROWS, LANES)


def from_rows(value):
    count = value.shape[0]
    return value.reshape(count, 8, 8, LANES).transpose(0, 2, 1, 3).reshape(count, 8, 8 * LANES)


def lane_of(shape):
    return lax.broadcasted_iota(jnp.int32, shape, len(shape) - 1)


def fill_padded(pad, place, source, index):
    for block in range(8):
        pad[place, FRONT + block] = source[index, 8 * block : 8 * block + 8, :]


def clear_margins(pad, count):
    nothing = jnp.zeros((8, LANES), jnp.float32)
    for place in range(count):
        for block in (0, 1, 10, 11, 12):
            pad[place, block] = nothing


def shifted(pad, place, delta):
    moved = delta + SMAX
    first = moved >> 2
    part = moved & 3
    turn = (LANES - 32 * part) & (LANES - 1)
    keep = lane_of((8, LANES)) < LANES - 32 * part
    rolled = [pltpu.roll(pad[place, first + block], turn, 1) for block in range(9)]
    return [jnp.where(keep, rolled[block], rolled[block + 1]) for block in range(8)]


def gather_fields(core, own_ref, swap_ref, next_ref, pad):
    for index in range(2):
        fill_padded(pad, 2 * core + index, own_ref, index)
        fill_padded(pad, 2 * (1 - core) + index, swap_ref, index)
        fill_padded(pad, 4 + index, next_ref, index)
    clear_margins(pad, 6)


def pre_kernel(table_ref, own_ref, swap_ref, next_ref, out_ref, pad):
    core = table_ref[2 * SLOTS]
    gather_fields(core, own_ref, swap_ref, next_ref, pad)
    for slot in range(SLOTS):
        moved = shifted(pad, table_ref[SLOTS + slot], table_ref[slot])
        for block in range(8):
            first = pad[slot // 2, FRONT + block]
            out_ref[slot // 2, slot % 2, 8 * block : 8 * block + 8, :] = FOURPI * (
                first * moved[block]
            )
    for index in range(2):
        out_ref[2 * core + index, 2] = own_ref[2 + index]
        out_ref[2 * (1 - core) + index, 2] = swap_ref[2 + index]


def post_kernel(
    table_ref, own_ref, swap_ref, next_ref, pot_ref, own_out, swap_out, next_out, pad, back, acc
):
    core = table_ref[2 * SLOTS]
    gather_fields(core, own_ref, swap_ref, next_ref, pad)
    clear_margins(back, 2)
    nothing = jnp.zeros((ROWS, LANES), jnp.float32)
    for place in range(6):
        acc[place] = nothing
    for slot in range(SLOTS):
        delta = table_ref[slot]
        place = table_ref[SLOTS + slot]
        live = table_ref[2 * SLOTS + 1 + slot] > 0
        moved = shifted(pad, place, delta)
        for block in range(8):
            rows = slice(8 * block, 8 * block + 8)
            value = jnp.where(live, pot_ref[slot // 2, slot % 2, rows, :], 0.0)
            acc[slot // 2, rows, :] = acc[slot // 2, rows, :] - value * moved[block]
            back[slot % 2, FRONT + block] = value * pad[slot // 2, FRONT + block]
        returned = shifted(back, slot % 2, -delta)
        for block in range(8):
            rows = slice(8 * block, 8 * block + 8)
            acc[place, rows, :] = acc[place, rows, :] - returned[block]
    for index in range(2):
        own_out[index] = acc[2 * core + index]
        swap_out[index] = acc[2 * (1 - core) + index]
        next_out[index] = acc[4 + index]


def roll(value, steps, axis):
    size = value.shape[axis]
    return pltpu.roll(value, steps % size, axis)


def exchange_groups(parts):
    lane = lane_of((8, LANES))
    low = lane < 64
    even = (lane & 32) == 0
    halves = [None] * 4
    for index in range(2):
        above, below = parts[index], parts[index + 2]
        crossed = roll(jnp.where(low, below, above), 64, 1)
        halves[index] = jnp.where(low, above, crossed)
        halves[index + 2] = jnp.where(low, crossed, below)
    result = [None] * 4
    for index in (0, 2):
        left, right = halves[index], halves[index + 1]
        result[index] = jnp.where(even, left, roll(right, 32, 1))
        result[index + 1] = jnp.where(even, roll(left, -32, 1), right)
    return result


class Level:
    def __init__(self, depth):
        self.zs = 8 >> depth
        self.ys = 4 >> depth
        self.step = 1 << depth
        lane = lane_of((8, LANES))
        sub = lax.broadcasted_iota(jnp.int32, (8, LANES), 0)
        column = lane & 31
        self.inside = (
            lane < 96,
            lane >= 32,
            sub < 7,
            sub > 0,
            column < 32 - self.step,
            column >= self.step,
        )

    def neighbours(self, get, q, r):
        ys = self.ys
        return (
            get(q + 1, r),
            get(q - 1, r),
            get(q, r + 1) if r < ys - 1 else roll(get(q, 0), -1, 0),
            get(q, r - 1) if r > 0 else roll(get(q, ys - 1), 1, 0),
            roll(get(q, r), -self.step, 1),
            roll(get(q, r), self.step, 1),
        )

    def wrapped(self, values):
        zs = self.zs

        def get(q, r):
            if q == zs:
                return roll(values[0, r], -32, 1)
            if q == -1:
                return roll(values[zs - 1, r], 32, 1)
            return values[q, r]

        return get

    def edges(self, q, r):
        return (
            self.inside[0] if q == self.zs - 1 else None,
            self.inside[1] if q == 0 else None,
            self.inside[2] if r == self.ys - 1 else None,
            self.inside[3] if r == 0 else None,
            self.inside[4],
            self.inside[5],
        )

    def coefficients(self, get, q, r):
        centre = get(q, r)
        edges = self.edges(q, r)
        around = [
            value if edge is None else jnp.where(edge, value, 0.0)
            for value, edge in zip(self.neighbours(get, q, r), edges)
        ]
        total = 6.0 * centre + sum(around[1:], around[0])
        scale = OMEGA / total
        couplings = []
        for value, edge in zip(around, edges):
            coupling = (centre + value) * scale
            couplings.append(coupling if edge is None else jnp.where(edge, coupling, 0.0))
        return couplings, total, scale

    def coupled(self, get, couplings, q, r):
        terms = [c * v for c, v in zip(couplings, self.neighbours(get, q, r))]
        return (terms[0] + terms[1]) + (terms[2] + terms[3]) + (terms[4] + terms[5])

    def pair_sum(self, value):
        even = (lane_of((8, LANES)) & self.step) == 0
        return value + jnp.where(even, roll(value, -self.step, 1), roll(value, self.step, 1))

    def block_sums(self, get):
        sums = {}
        for q in range(0, self.zs, 2):
            for r in range(0, self.ys, 2):
                four = (get(q, r) + get(q, r + 1)) + (get(q + 1, r) + get(q + 1, r + 1))
                sums[q // 2, r // 2] = self.pair_sum(four)
        return sums

    def cells(self):
        return [(q, r) for q in range(self.zs) for r in range(self.ys)]


def solve_kernel(in_ref, out_ref, eps, couple, total, source, field, half_ref, quarter_ref):
    fine, half, quarter = Level(0), Level(1), Level(2)
    slots = (0, 1)

    def place(q, r):
        return (q + 1) * 4 + r

    def at(ref, *lead):
        return lambda q, r: ref[(*lead, place(q, r))]

    def close_ends(ref, *lead):
        for r in range(4):
            ref[(*lead, place(8, r))] = roll(ref[(*lead, place(0, r))], -32, 1)
            ref[(*lead, place(-1, r))] = roll(ref[(*lead, place(7, r))], 32, 1)

    for q in range(8):
        for which in range(3):
            parts = [in_ref[part, which, pl.ds(q, 8, stride=8), :] for part in range(4)]
            turned = exchange_groups(parts)
            for r in range(4):
                if which == 2:
                    eps[place(q, r)] = turned[r]
                else:
                    source[which, q * 4 + r] = turned[r]
    close_ends(eps)

    get_eps = at(eps)
    for q, r in fine.cells():
        couplings, summed, scale = fine.coefficients(get_eps, q, r)
        for side in range(6):
            couple[side, q * 4 + r] = couplings[side]
        total[q * 4 + r] = summed
        for slot in slots:
            started = (2.0 * scale) * source[slot, q * 4 + r]
            source[slot, q * 4 + r] = started
            field[0, slot, place(q, r)] = started
    for slot in slots:
        close_ends(field, 0, slot)

    def keep_level(level, ref, eps_level):
        get = level.wrapped(eps_level)
        for q, r in level.cells():
            couplings, summed, scale = level.coefficients(get, q, r)
            for side in range(6):
                ref[side, q * level.ys + r] = couplings[side]
            ref[6, q * level.ys + r] = summed
            ref[7, q * level.ys + r] = 0.625 * scale

    def means(level, get):
        return {key: 0.125 * value for key, value in level.block_sums(get).items()}

    eps_half = means(fine, get_eps)
    keep_level(half, half_ref, eps_half)
    keep_level(quarter, quarter_ref, means(half, lambda q, r: eps_half[q, r]))

    def kept(level, ref, item, q, r):
        return ref[item, q * level.ys + r]

    def around(level, ref, values, q, r):
        couplings = [kept(level, ref, side, q, r) for side in range(6)]
        return level.coupled(level.wrapped(values), couplings, q, r)

    def relaxed(level, ref, values, rhs):
        return {
            (q, r): ((1.0 - OMEGA) * values[q, r] + rhs[q, r]) + around(level, ref, values, q, r)
            for q, r in level.cells()
        }

    def correction(rhs):
        def weighted(q, r):
            return kept(half, half_ref, 6, q, r) * (
                (1.0 - OMEGA) * rhs[q, r] + around(half, half_ref, rhs, q, r)
            )

        sums = half.block_sums(weighted)
        start = {key: kept(quarter, quarter_ref, 7, *key) * sums[key] for key in quarter.cells()}
        lowest = start
        for _ in range(SWEEPS - 1):
            lowest = relaxed(quarter, quarter_ref, lowest, start)
        values = {(q, r): rhs[q, r] + lowest[q // 2, r // 2] for q, r in half.cells()}
        return relaxed(half, half_ref, values, rhs)

    def fine_coupled(couplings, lead, q, r):
        return fine.coupled(at(field, *lead), couplings, q, r)

    def fine_couplings(q, r):
        return [couple[side, q * 4 + r] for side in range(6)]

    def correct():
        rhs = ({}, {})
        for q in range(0, 8, 2):
            for r in range(0, 4, 2):
                four = [None, None]
                for qq, rr in ((q, r), (q, r + 1), (q + 1, r), (q + 1, r + 1)):
                    couplings = fine_couplings(qq, rr)
                    for slot in slots:
                        left = source[slot, qq * 4 + rr] - OMEGA * field[0, slot, place(qq, rr)]
                        left = left + fine_coupled(couplings, (0, slot), qq, rr)
                        term = total[qq * 4 + rr] * left
                        four[slot] = term if four[slot] is None else four[slot] + term
                key = (q // 2, r // 2)
                for slot in slots:
                    rhs[slot][key] = kept(half, half_ref, 7, *key) * fine.pair_sum(four[slot])
        extra = [correction(rhs[slot]) for slot in slots]
        for slot in slots:
            for q, r in fine.cells():
                corrected = field[0, slot, place(q, r)] + extra[slot][q // 2, r // 2]
                field[0, slot, place(q, r)] = corrected
            close_ends(field, 0, slot)

    def relax(before, after):
        for q, r in fine.cells():
            couplings = fine_couplings(q, r)
            for slot in slots:
                value = (1.0 - OMEGA) * field[before, slot, place(q, r)]
                value = value + source[slot, q * 4 + r]
                value = value + fine_coupled(couplings, (before, slot), q, r)
                field[after, slot, place(q, r)] = value
        for slot in slots:
            close_ends(field, after, slot)

    def cycle(index, carry):
        correct()
        relax(0, 1)

        @pl.when(index < CYCLES - 1)
        def _():
            relax(1, 0)

        return carry

    lax.fori_loop(0, CYCLES, cycle, 0)
    for q in range(8):
        for slot in slots:
            turned = exchange_groups([field[1, slot, place(q, r)] for r in range(4)])
            for part in range(4):
                out_ref[part, slot, pl.ds(q, 8, stride=8), :] = turned[part]


def near(value):
    return pltpu.with_memory_space_constraint(value, pltpu.VMEM)


def in_scalars(value):
    return pltpu.with_memory_space_constraint(value, pltpu.SMEM)


def fill_table(owner, offsets_ref, counts_ref, shift_ref, table_ref):
    core = owner & 1
    base = 2 * (owner - core)
    orbital_count = counts_ref.shape[0]
    for slot in range(SLOTS):
        first = slot // 2
        second = jnp.where(core == 0, SECOND[0][slot], SECOND[1][slot])
        other = base + second
        other = jnp.where(other >= orbital_count, other - orbital_count, other)
        table_ref[slot] = shift_ref[base + first] - shift_ref[other]
        table_ref[SLOTS + slot] = jnp.where(core == 0, PLACE[0][slot], PLACE[1][slot])
        count = counts_ref[base + first]
        live = jnp.int32(0)
        for rank in range(PMAX):
            listed = (count > rank) & (offsets_ref[rank, base + first] + 1 == second - first)
            live = live + listed.astype(jnp.int32)
        table_ref[2 * SLOTS + 1 + slot] = live
    table_ref[2 * SLOTS] = core


def prepare_kernel(
    own_hbm, eps_hbm, offsets_hbm, counts_hbm, shift_hbm,
    packet_ref, table_ref,
    offsets_ref, counts_ref, shift_ref, sems,
):
    copies = [
        pltpu.make_async_copy(offsets_hbm, offsets_ref, sems.at[0]),
        pltpu.make_async_copy(counts_hbm, counts_ref, sems.at[1]),
        pltpu.make_async_copy(shift_hbm, shift_ref, sems.at[2]),
        pltpu.make_async_copy(own_hbm, packet_ref.at[0:2], sems.at[3]),
        pltpu.make_async_copy(eps_hbm, packet_ref.at[2:4], sems.at[4]),
    ]
    for copy in copies:
        copy.start()
    for copy in copies[:3]:
        copy.wait()
    fill_table(lax.axis_index("orb"), offsets_ref, counts_ref, shift_ref, table_ref)
    for copy in copies[3:]:
        copy.wait()


def shards(orbitals, dielectric, pair_offsets, pair_counts, box_shift):
    owners = lax.axis_size("orb")
    swapped = [(source, source ^ 1) for source in range(owners)]
    back_chip = [(source, (source - 2) % owners) for source in range(owners)]
    next_chip = [(source, (source + 2) % owners) for source in range(owners)]

    own = as_rows(orbitals)
    eps = as_rows(dielectric)
    beyond = lax.ppermute(own, "orb", back_chip)
    smem = pl.BlockSpec(memory_space=pltpu.SMEM)
    vmem = pl.BlockSpec(memory_space=pltpu.VMEM)
    anywhere = pl.BlockSpec(memory_space=pl.ANY)
    count = pair_counts.shape[0]
    packet, table = pl.pallas_call(
        prepare_kernel,
        out_shape=(
            pltpu.VMEM((4, ROWS, LANES), jnp.float32),
            pltpu.SMEM((3 * SLOTS + 1,), jnp.int32),
        ),
        in_specs=[anywhere] * 5,
        out_specs=(vmem, smem),
        scratch_shapes=[
            pltpu.SMEM((PMAX, count), jnp.int32),
            pltpu.SMEM((count,), jnp.int32),
            pltpu.SMEM((count,), jnp.int32),
            pltpu.SemaphoreType.DMA((5,)),
        ],
        name="pair_prepare",
    )(own, eps, pair_offsets.T, pair_counts, box_shift)
    table = in_scalars(table)
    across = lax.ppermute(packet, "orb", swapped)
    pad_scratch = pltpu.VMEM((6, PADDED, 8, LANES), jnp.float32)
    requests = pl.pallas_call(
        pre_kernel,
        out_shape=pltpu.VMEM((4, 3, ROWS, LANES), jnp.float32),
        in_specs=[smem, vmem, vmem, vmem],
        out_specs=vmem,
        scratch_shapes=[pad_scratch],
        name="pair_sources",
    )(table, near(packet), near(across), near(beyond))
    arrived = lax.all_to_all(requests, "grid", 0, 0)
    cells = (32, 8, LANES)
    ended = (40, 8, LANES)
    potentials = pl.pallas_call(
        solve_kernel,
        out_shape=pltpu.VMEM((4, 2, ROWS, LANES), jnp.float32),
        in_specs=[vmem],
        out_specs=vmem,
        scratch_shapes=[
            pltpu.VMEM(ended, jnp.float32),
            pltpu.VMEM((6, *cells), jnp.float32),
            pltpu.VMEM(cells, jnp.float32),
            pltpu.VMEM((2, *cells), jnp.float32),
            pltpu.VMEM((2, 2, *ended), jnp.float32),
            pltpu.VMEM((8, 8, 8, LANES), jnp.float32),
            pltpu.VMEM((8, 2, 8, LANES), jnp.float32),
        ],
        name="pair_solve",
    )(near(arrived))
    returned = lax.all_to_all(potentials, "grid", 0, 0)
    two = pltpu.VMEM((2, ROWS, LANES), jnp.float32)
    mine, theirs, later = pl.pallas_call(
        post_kernel,
        out_shape=(two, two, two),
        in_specs=[smem, vmem, vmem, vmem, vmem],
        out_specs=(vmem, vmem, vmem),
        scratch_shapes=[
            pad_scratch,
            pltpu.VMEM((2, PADDED, 8, LANES), jnp.float32),
            pltpu.VMEM((6, ROWS, LANES), jnp.float32),
        ],
        name="pair_actions",
    )(table, near(packet), near(across), near(beyond), near(returned))
    from_before = lax.ppermute(later, "orb", next_chip)
    from_chip = lax.ppermute(theirs, "orb", swapped)
    return from_rows(mine + from_chip + from_before)


def solution(mesh):
    placed = (P("orb", "grid", None), P("orb", "grid", None), P(), P(), P())
    return jax.shard_map(
        shards, mesh=mesh, in_specs=placed, out_specs=P("orb", "grid", None), check_vma=False
    )
```

time: 60.7 us -> 58.4 us (0.962)
  waiting for transfers between devices: 6.92 us -> 9.36 us
  other arithmetic: 2.66 us -> 0.64 us
  Pallas kernels: 6.49 us -> 5.28 us
  blocking collectives: 19.6 us -> 18.7 us
  local copies, waits for them, and re-layouts: 0.9 us -> 0.01 us
    ppermute x1, starting transfers between devices: 14.4 us -> 8.23 us  [shards(): beyond = lax.ppermute(own, 'orb', back_chip)]
    ppermute x1, starting transfers between devices: 3 us -> 8.75 us  [shards(): across = lax.ppermute(packet, 'orb', swapped)]
    concatenate x3 -> x0, other arithmetic: 1.56 us -> none  [the longest x1 0.93 us: shards(): across = lax.ppermute(jnp.concatenate([own, eps]), 'orb', swapped)]
    ppermute x1, waiting for transfers between devices: 0.01 us -> 1.41 us  [shards(): beyond = lax.ppermute(own, 'orb', back_chip)]
    pallas_call x0 -> x1, Pallas kernels: none -> 1.07 us  [shards(): pl.pallas_call(prepare_kernel, out_shape=(pltpu.VMEM((4, ROWS, LANES), jn...]
    ppermute x1, waiting for transfers between devices: 6.91 us -> 7.94 us  [shards(): from_before = lax.ppermute(later, 'orb', next_chip)]
    pallas_call x1, Pallas kernels: 4.72 us -> 3.77 us  [shards(): pl.pallas_call(solve_kernel, out_shape=pltpu.VMEM((4, 2, ROWS, LANES), jn...]
    ppermute x1, starting transfers between devices: 4.21 us -> 5.07 us  [shards(): from_chip = lax.ppermute(theirs, 'orb', swapped)]
  transfers between devices with their start and end apart: 4 -> 4, of which waited for: 1 -> 2; matrix products, arithmetic and copies ran while one was open for 5% -> 0% of each run, Pallas kernels for 0% -> 0%
where the time goes in v2:
time: 58.4 us; the launch traced here: 58.1 us
  starting transfers between devices  24 us (41%)
  blocking collectives  18.7 us (32%)
  waiting for transfers between devices  9.36 us (16%)
  Pallas kernels  5.28 us (9%)
  other arithmetic  0.64 us (1%)
    all_to_all x1, blocking collectives, shards(): arrived = lax.all_to_all(requests, 'grid', 0, 0)  10.8 us
    ppermute x1, starting transfers between devices, shards(): across = lax.ppermute(packet, 'orb', swapped)  8.75 us
    ppermute x1, starting transfers between devices, shards(): beyond = lax.ppermute(own, 'orb', back_chip)  8.23 us
    ppermute x1, waiting for transfers between devices, shards(): from_before = lax.ppermute(later, 'orb', next_chip)  7.94 us
    all_to_all x1, blocking collectives, shards(): returned = lax.all_to_all(potentials, 'grid', 0, 0)  7.92 us
    ppermute x1, starting transfers between devices, shards(): from_chip = lax.ppermute(theirs, 'orb', swapped)  5.07 us
    pallas_call x1, Pallas kernels, shards(): pl.pallas_call(solve_kernel, out_shape=pltpu.VMEM((4, 2, ROWS, LANES), jn...  3.77 us
    ppermute x1, starting transfers between devices, shards(): from_before = lax.ppermute(later, 'orb', next_chip)  1.92 us
  transfers between devices with their start and end apart: 4, of which 2 were waited for; matrix products, arithmetic and copies ran while one was open for 0% of the time, Pallas kernels for 0%

profile of v2, /device:TPU:1, one launch (start us, length us, event | category | flops | bytes accessed | tf_op | source)
XLA Modules:
  0.0 58.1 jit_solution(2589865876387749718)
XLA Ops:
  0.0 0.0 copy-start
  0.0 1.1 %pair_prepare.1 = (f32[4,64,128]{2,1,0:T(8,128)S(1)}, s32[25]{0:T(128)S(4)}) custom-call(f32[2,64,128]{2,1,0:T(8,128)} %bitcast.18, f32[2,64,128]{2,1,0:T(8,128)} %bitcast.17, s32[4,256]{1,0:T(4,128)} %bitcast.20, s32[256]{0:T(256)} %counts_hbm.1, s32[256]{0:T(256)} %shift_hbm.1), custom_call_target="tpu_custom_call" | custom-call | tf_op jit(solution)/shard_map/pair_prepare/pallas_call | solution.py:421
  1.1 8.7 %collective-permute-start = (f32[4,64,128]{2,1,0:T(8,128)S(1)}, f32[4,64,128]{2,1,0:T(8,128)S(1)}, u32[]{:S(2)}, u32[]{:S(2)}) collective-permute-start(f32[4,64,128]{2,1,0:T(8,128)S(1)} %get-tuple-element.11.own_ref), channel_id=1, source_target_pairs={{0,4},{4,0},{8,12},{12,8},{16,20},{20,16},{24,28},{28,24},{32,36},... | collective-permute-start | bytes 393224 | tf_op jit(solution)/shard_map/ppermute | solution.py:438
  9.8 0.0 copy-done
  9.8 8.2 %collective-permute-start.1 = (f32[2,64,128]{2,1,0:T(8,128)S(1)}, f32[2,64,128]{2,1,0:T(8,128)S(1)}, u32[]{:S(2)}, u32[]{:S(2)}) collective-permute-start(f32[2,64,128]{2,1,0:T(8,128)S(1)} %bitcast.19), channel_id=1, source_target_pairs={{0,504},{4,508},{8,0},{12,4},{16,8},{20,12},{24,16},{28,20},{32,24... | collective-permute-start | bytes 196616 | tf_op jit(solution)/shard_map/ppermute | solution.py:416
  18.1 1.4 %collective-permute-done.1.next_ref = f32[2,64,128]{2,1,0:T(8,128)S(1)} collective-permute-done((f32[2,64,128]{2,1,0:T(8,128)S(1)}, f32[2,64,128]{2,1,0:T(8,128)S(1)}, u32[]{:S(2)}, u32[]{:S(2)}) %collective-permute-start.1) | collective-permute-done | bytes 65568 | tf_op jit(solution)/shard_map/ppermute | solution.py:416
  19.5 0.0 collective-permute-done.swap_ref
  19.5 0.2 pair_sources.1
  19.7 10.8 %all_to_all.10.in_ref = f32[4,3,64,128]{3,2,1,0:T(8,128)S(1)} all-to-all(f32[4,3,64,128]{3,2,1,0:T(8,128)S(1)} %pair_sources.1), channel_id=1, replica_groups=mesh['orb'=128,'grid'=4] {'grid'}, dimensions={0} | all-to-all | bytes 786432 | tf_op jit(solution)/shard_map/all_to_all | solution.py:448
  30.5 3.8 %pair_solve.1 = f32[4,2,64,128]{3,2,1,0:T(8,128)S(1)} custom-call(f32[4,3,64,128]{3,2,1,0:T(8,128)S(1)} %all_to_all.10.in_ref), custom_call_target="tpu_custom_call" | custom-call | tf_op jit(solution)/shard_map/pair_solve/pallas_call | solution.py:451
  34.3 7.9 %all_to_all.11.pot_ref = f32[4,2,64,128]{3,2,1,0:T(8,128)S(1)} all-to-all(f32[4,2,64,128]{3,2,1,0:T(8,128)S(1)} %pair_solve.1), channel_id=1, replica_groups=mesh['orb'=128,'grid'=4] {'grid'}, dimensions={0} | all-to-all | bytes 524288 | tf_op jit(solution)/shard_map/all_to_all | solution.py:467
  42.2 0.3 pair_actions.1
  42.5 5.1 %collective-permute-start.2 = (f32[2,64,128]{2,1,0:T(8,128)S(1)}, f32[2,64,128]{2,1,0:T(8,128)S(1)}, u32[]{:S(2)}, u32[]{:S(2)}) collective-permute-start(f32[2,64,128]{2,1,0:T(8,128)S(1)} %get-tuple-element.13), channel_id=1, source_target_pairs={{0,4},{4,0},{8,12},{12,8},{16,20},{20,16},{24,28},{28,24},{32,36},... | collective-permute-start | bytes 196616 | tf_op jit(solution)/shard_map/ppermute | solution.py:482
  47.6 1.9 %collective-permute-start.3 = (f32[2,64,128]{2,1,0:T(8,128)S(1)}, f32[2,64,128]{2,1,0:T(8,128)S(1)}, u32[]{:S(2)}, u32[]{:S(2)}) collective-permute-start(f32[2,64,128]{2,1,0:T(8,128)S(1)} %get-tuple-element.14), channel_id=1, source_target_pairs={{0,8},{4,12},{8,16},{12,20},{16,24},{20,28},{24,32},{28,36},{32,40... | collective-permute-start | bytes 196616 | tf_op jit(solution)/shard_map/ppermute | solution.py:481
  49.5 0.0 collective-permute-done.2
  49.5 7.9 %collective-permute-done.3 = f32[2,64,128]{2,1,0:T(8,128)S(1)} collective-permute-done((f32[2,64,128]{2,1,0:T(8,128)S(1)}, f32[2,64,128]{2,1,0:T(8,128)S(1)}, u32[]{:S(2)}, u32[]{:S(2)}) %collective-permute-start.3) | collective-permute-done | bytes 65568 | tf_op jit(solution)/shard_map/ppermute | solution.py:481
  57.4 0.6 %add_bitcast_fusion = f32[2,8,1024]{2,1,0:T(8,128)} fusion(f32[2,64,128]{2,1,0:T(8,128)S(1)} %collective-permute-done.3, f32[2,64,128]{2,1,0:T(8,128)S(1)} %get-tuple-element.12, f32[2,64,128]{2,1,0:T(8,128)S(1)} %collective-permute-done.2), kind=kLoop, calls=%fused_computation | loop fusion | flops 32768 | bytes 262144 | tf_op jit(solution)/shard_map/reshape | solution.py:31
Async XLA Ops:
  0.0 9.8 %copy-start = (f32[2,8,1024]{2,1,0:T(8,128)S(1)}, f32[2,8,1024]{2,1,0:T(8,128)}, u32[]{:S(2)}) copy-start(f32[2,8,1024]{2,1,0:T(8,128)} %param.5) | copy-start | bytes 196612
  1.1 18.4 %collective-permute-start = (f32[4,64,128]{2,1,0:T(8,128)S(1)}, f32[4,64,128]{2,1,0:T(8,128)S(1)}, u32[]{:S(2)}, u32[]{:S(2)}) collective-permute-start(f32[4,64,128]{2,1,0:T(8,128)S(1)} %get-tuple-element.11.own_ref), channel_id=1, source_target_pairs={{0,4},{4,0},{8,12},{12,8},{16,20},{20,16},{24,28},{28,24},{32,36},... | collective-permute-start | bytes 393224 | tf_op jit(solution)/shard_map/ppermute | solution.py:438
  9.8 9.6 %collective-permute-start.1 = (f32[2,64,128]{2,1,0:T(8,128)S(1)}, f32[2,64,128]{2,1,0:T(8,128)S(1)}, u32[]{:S(2)}, u32[]{:S(2)}) collective-permute-start(f32[2,64,128]{2,1,0:T(8,128)S(1)} %bitcast.19), channel_id=1, source_target_pairs={{0,504},{4,508},{8,0},{12,4},{16,8},{20,12},{24,16},{28,20},{32,24... | collective-permute-start | bytes 196616 | tf_op jit(solution)/shard_map/ppermute | solution.py:416
  42.5 7.0 %collective-permute-start.2 = (f32[2,64,128]{2,1,0:T(8,128)S(1)}, f32[2,64,128]{2,1,0:T(8,128)S(1)}, u32[]{:S(2)}, u32[]{:S(2)}) collective-permute-start(f32[2,64,128]{2,1,0:T(8,128)S(1)} %get-tuple-element.13), channel_id=1, source_target_pairs={{0,4},{4,0},{8,12},{12,8},{16,20},{20,16},{24,28},{28,24},{32,36},... | collective-permute-start | bytes 196616 | tf_op jit(solution)/shard_map/ppermute | solution.py:482
  47.6 9.9 %collective-permute-start.3 = (f32[2,64,128]{2,1,0:T(8,128)S(1)}, f32[2,64,128]{2,1,0:T(8,128)S(1)}, u32[]{:S(2)}, u32[]{:S(2)}) collective-permute-start(f32[2,64,128]{2,1,0:T(8,128)S(1)} %get-tuple-element.14), channel_id=1, source_target_pairs={{0,8},{4,12},{8,16},{12,20},{16,24},{20,28},{24,32},{28,36},{32,40... | collective-permute-start | bytes 196616 | tf_op jit(solution)/shard_map/ppermute | solution.py:481

commit v3 on v2

--- a/solution.py
+++ b/solution.py
@@ -12,9 +12,10 @@
 FOURPI = 4.0 * 3.141592653589793
 OMEGA = 0.8
 
-SECOND = ((1, 4, 4, 5, 4, 5, 4, 5), (2, 3, 2, 3, 3, 6, 6, 7))
-PLACE = ((1, 4, 4, 5, 4, 5, 4, 5), (2, 3, 2, 3, 3, 4, 4, 5))
 SLOTS = 8
+ONE = ((0, 0, 1, 1, 2, 2, 3, 3), (0, 0, 0, 0, 1, 1, 1, 1))
+OTHER = ((1, 2, 2, 3, 4, 5, 4, 5), (1, 2, 3, 4, 2, 3, 4, 5))
+DELTA, FIRST, SECOND, LIVE, CORE = 0, SLOTS, 2 * SLOTS, 3 * SLOTS, 4 * SLOTS
 FRONT = 2
 PADDED = 13
 ROWS = 64
@@ -57,56 +58,57 @@
     return [jnp.where(keep, rolled[block], rolled[block + 1]) for block in range(8)]
 
 
-def gather_fields(core, own_ref, swap_ref, next_ref, pad):
+def gather_fields(core, before_ref, across_ref, own_ref, pad):
     for index in range(2):
-        fill_padded(pad, 2 * core + index, own_ref, index)
-        fill_padded(pad, 2 * (1 - core) + index, swap_ref, index)
-        fill_padded(pad, 4 + index, next_ref, index)
+        fill_padded(pad, index, before_ref, index)
+        fill_padded(pad, 2 + 2 * core + index, own_ref, index)
+        fill_padded(pad, 4 - 2 * core + index, across_ref, index)
     clear_margins(pad, 6)
 
 
-def pre_kernel(table_ref, own_ref, swap_ref, next_ref, out_ref, pad):
-    core = table_ref[2 * SLOTS]
-    gather_fields(core, own_ref, swap_ref, next_ref, pad)
+def pre_kernel(table_ref, before_ref, across_ref, own_ref, out_ref, pad):
+    core = table_ref[CORE]
+    gather_fields(core, before_ref, across_ref, own_ref, pad)
     for slot in range(SLOTS):
-        moved = shifted(pad, table_ref[SLOTS + slot], table_ref[slot])
+        one, other = table_ref[FIRST + slot], table_ref[SECOND + slot]
+        moved = shifted(pad, other, table_ref[DELTA + slot])
         for block in range(8):
-            first = pad[slot // 2, FRONT + block]
             out_ref[slot // 2, slot % 2, 8 * block : 8 * block + 8, :] = FOURPI * (
-                first * moved[block]
+                pad[one, FRONT + block] * moved[block]
             )
-    for index in range(2):
-        out_ref[2 * core + index, 2] = own_ref[2 + index]
-        out_ref[2 * (1 - core) + index, 2] = swap_ref[2 + index]
+    out_ref[0, 2] = before_ref[2]
+    out_ref[1, 2] = before_ref[3 - core]
+    out_ref[2, 2] = jnp.where(core == 0, own_ref[2], before_ref[3])
+    out_ref[3, 2] = jnp.where(core == 0, own_ref[3], before_ref[3])
 
 
 def post_kernel(
-    table_ref, own_ref, swap_ref, next_ref, pot_ref, own_out, swap_out, next_out, pad, back, acc
+    table_ref, before_ref, across_ref, own_ref, pot_ref, before_out, across_out, own_out, pad, back, acc
 ):
-    core = table_ref[2 * SLOTS]
-    gather_fields(core, own_ref, swap_ref, next_ref, pad)
+    core = table_ref[CORE]
+    gather_fields(core, before_ref, across_ref, own_ref, pad)
     clear_margins(back, 2)
     nothing = jnp.zeros((ROWS, LANES), jnp.float32)
     for place in range(6):
         acc[place] = nothing
     for slot in range(SLOTS):
-        delta = table_ref[slot]
-        place = table_ref[SLOTS + slot]
-        live = table_ref[2 * SLOTS + 1 + slot] > 0
-        moved = shifted(pad, place, delta)
+        delta = table_ref[DELTA + slot]
+        one, other = table_ref[FIRST + slot], table_ref[SECOND + slot]
+        live = table_ref[LIVE + slot] > 0
+        moved = shifted(pad, other, delta)
         for block in range(8):
             rows = slice(8 * block, 8 * block + 8)
             value = jnp.where(live, pot_ref[slot // 2, slot % 2, rows, :], 0.0)
-            acc[slot // 2, rows, :] = acc[slot // 2, rows, :] - value * moved[block]
-            back[slot % 2, FRONT + block] = value * pad[slot // 2, FRONT + block]
+            acc[one, rows, :] = acc[one, rows, :] - value * moved[block]
+            back[slot % 2, FRONT + block] = value * pad[one, FRONT + block]
         returned = shifted(back, slot % 2, -delta)
         for block in range(8):
             rows = slice(8 * block, 8 * block + 8)
-            acc[place, rows, :] = acc[place, rows, :] - returned[block]
+            acc[other, rows, :] = acc[other, rows, :] - returned[block]
     for index in range(2):
-        own_out[index] = acc[2 * core + index]
-        swap_out[index] = acc[2 * (1 - core) + index]
-        next_out[index] = acc[4 + index]
+        before_out[index] = acc[index]
+        own_out[index] = acc[2 + 2 * core + index]
+        across_out[index] = acc[4 - 2 * core + index]
 
 
 def roll(value, steps, axis):
@@ -365,23 +367,29 @@
 
 
 def fill_table(owner, offsets_ref, counts_ref, shift_ref, table_ref):
+    orbital_count = counts_ref.shape[0]
     core = owner & 1
-    base = 2 * (owner - core)
-    orbital_count = counts_ref.shape[0]
+    base = 2 * (owner - core) - 4
+
+    def orbital_of(place):
+        orbital = base + jnp.where(place < 2, 2 * core, 2) + place
+        return jnp.where(orbital < 0, orbital + orbital_count, orbital)
+
     for slot in range(SLOTS):
-        first = slot // 2
-        second = jnp.where(core == 0, SECOND[0][slot], SECOND[1][slot])
-        other = base + second
-        other = jnp.where(other >= orbital_count, other - orbital_count, other)
-        table_ref[slot] = shift_ref[base + first] - shift_ref[other]
-        table_ref[SLOTS + slot] = jnp.where(core == 0, PLACE[0][slot], PLACE[1][slot])
-        count = counts_ref[base + first]
+        one = jnp.where(core == 0, ONE[0][slot], ONE[1][slot])
+        other = jnp.where(core == 0, OTHER[0][slot], OTHER[1][slot])
+        first, second = orbital_of(one), orbital_of(other)
+        gap = second - first
+        gap = jnp.where(gap < 0, gap + orbital_count, gap)
         live = jnp.int32(0)
         for rank in range(PMAX):
-            listed = (count > rank) & (offsets_ref[rank, base + first] + 1 == second - first)
+            listed = (counts_ref[first] > rank) & (offsets_ref[rank, first] + 1 == gap)
             live = live + listed.astype(jnp.int32)
-        table_ref[2 * SLOTS + 1 + slot] = live
-    table_ref[2 * SLOTS] = core
+        table_ref[DELTA + slot] = shift_ref[first] - shift_ref[second]
+        table_ref[FIRST + slot] = one
+        table_ref[SECOND + slot] = other
+        table_ref[LIVE + slot] = live
+    table_ref[CORE] = core
 
 
 def prepare_kernel(
@@ -407,13 +415,13 @@
 
 def shards(orbitals, dielectric, pair_offsets, pair_counts, box_shift):
     owners = lax.axis_size("orb")
+
     swapped = [(source, source ^ 1) for source in range(owners)]
-    back_chip = [(source, (source - 2) % owners) for source in range(owners)]
-    next_chip = [(source, (source + 2) % owners) for source in range(owners)]
+    onward = [(source, (source + 2) % owners) for source in range(owners)]
+    backward = [(source, (source - 2) % owners) for source in range(owners)]
 
     own = as_rows(orbitals)
     eps = as_rows(dielectric)
-    beyond = lax.ppermute(own, "orb", back_chip)
     smem = pl.BlockSpec(memory_space=pltpu.SMEM)
     vmem = pl.BlockSpec(memory_space=pltpu.VMEM)
     anywhere = pl.BlockSpec(memory_space=pl.ANY)
@@ -422,7 +430,7 @@
         prepare_kernel,
         out_shape=(
             pltpu.VMEM((4, ROWS, LANES), jnp.float32),
-            pltpu.SMEM((3 * SLOTS + 1,), jnp.int32),
+            pltpu.SMEM((4 * SLOTS + 1,), jnp.int32),
         ),
         in_specs=[anywhere] * 5,
         out_specs=(vmem, smem),
@@ -435,7 +443,8 @@
         name="pair_prepare",
     )(own, eps, pair_offsets.T, pair_counts, box_shift)
     table = in_scalars(table)
-    across = lax.ppermute(packet, "orb", swapped)
+    before = lax.ppermute(packet, "orb", onward)
+    across = lax.ppermute(own, "orb", swapped)
     pad_scratch = pltpu.VMEM((6, PADDED, 8, LANES), jnp.float32)
     requests = pl.pallas_call(
         pre_kernel,
@@ -444,7 +453,7 @@
         out_specs=vmem,
         scratch_shapes=[pad_scratch],
         name="pair_sources",
-    )(table, near(packet), near(across), near(beyond))
+    )(table, near(before), near(across), near(packet))
     arrived = lax.all_to_all(requests, "grid", 0, 0)
     cells = (32, 8, LANES)
     ended = (40, 8, LANES)
@@ -466,7 +475,7 @@
     )(near(arrived))
     returned = lax.all_to_all(potentials, "grid", 0, 0)
     two = pltpu.VMEM((2, ROWS, LANES), jnp.float32)
-    mine, theirs, later = pl.pallas_call(
+    for_before, for_across, mine = pl.pallas_call(
         post_kernel,
         out_shape=(two, two, two),
         in_specs=[smem, vmem, vmem, vmem, vmem],
@@ -477,10 +486,10 @@
             pltpu.VMEM((6, ROWS, LANES), jnp.float32),
         ],
         name="pair_actions",
-    )(table, near(packet), near(across), near(beyond), near(returned))
-    from_before = lax.ppermute(later, "orb", next_chip)
-    from_chip = lax.ppermute(theirs, "orb", swapped)
-    return from_rows(mine + from_chip + from_before)
+    )(table, near(before), near(across), near(packet), near(returned))
+    from_next = lax.ppermute(for_before, "orb", backward)
+    from_across = lax.ppermute(for_across, "orb", swapped)
+    return from_rows(mine + from_across + from_next)
 
 
 def solution(mesh):

time: 58.4 us -> 53.2 us (0.911)
  starting transfers between devices: 24 us -> 19.7 us
  blocking collectives: 18.7 us -> 18.1 us
    ppermute x4, starting transfers between devices: 24 us -> 19.7 us  [the longest x1 6.64 us: shards(): across = lax.ppermute(own, 'orb', swapped)]
    all_to_all x1, blocking collectives: 10.8 us -> 10.2 us  [shards(): arrived = lax.all_to_all(requests, 'grid', 0, 0)]
  transfers between devices with their start and end apart: 4 -> 4, of which waited for: 2 -> 3; matrix products, arithmetic and copies ran while one was open for 0% -> 0% of each run, Pallas kernels for 0% -> 0%
where the time goes in v3:
time: 53.2 us; the launch traced here: 52.9 us
  starting transfers between devices  19.7 us (37%)
  blocking collectives  18.1 us (34%)
  waiting for transfers between devices  9.16 us (17%)
  Pallas kernels  5.3 us (10%)
  other arithmetic  0.64 us (1%)
    all_to_all x1, blocking collectives, shards(): arrived = lax.all_to_all(requests, 'grid', 0, 0)  10.2 us
    all_to_all x1, blocking collectives, shards(): returned = lax.all_to_all(potentials, 'grid', 0, 0)  7.92 us
    ppermute x1, starting transfers between devices, shards(): across = lax.ppermute(own, 'orb', swapped)  6.64 us
    ppermute x1, waiting for transfers between devices, shards(): before = lax.ppermute(packet, 'orb', onward)  6.01 us
    ppermute x1, starting transfers between devices, shards(): from_across = lax.ppermute(for_across, 'orb', swapped)  5.74 us
    ppermute x1, starting transfers between devices, shards(): before = lax.ppermute(packet, 'orb', onward)  4.02 us
    pallas_call x1, Pallas kernels, shards(): pl.pallas_call(solve_kernel, out_shape=pltpu.VMEM((4, 2, ROWS, LANES), jn...  3.77 us
    ppermute x1, starting transfers between devices, shards(): from_next = lax.ppermute(for_before, 'orb', backward)  3.24 us
  transfers between devices with their start and end apart: 4, of which 3 were waited for; matrix products, arithmetic and copies ran while one was open for 0% of the time, Pallas kernels for 0%

profile of v3, /device:TPU:1, one launch (start us, length us, event | category | flops | bytes accessed | tf_op | source)
XLA Modules:
  0.0 52.9 jit_solution(4982657341394901629)
XLA Ops:
  0.0 0.0 copy-start
  0.0 1.1 %pair_prepare.1 = (f32[4,64,128]{2,1,0:T(8,128)S(1)}, s32[33]{0:T(128)S(4)}) custom-call(f32[2,64,128]{2,1,0:T(8,128)} %bitcast.18, f32[2,64,128]{2,1,0:T(8,128)} %bitcast.17, s32[4,256]{1,0:T(4,128)} %bitcast.20, s32[256]{0:T(256)} %counts_hbm.1, s32[256]{0:T(256)} %shift_hbm.1), custom_call_target="tpu_custom_call" | custom-call | tf_op jit(solution)/shard_map/pair_prepare/pallas_call | solution.py:429
  1.1 4.0 %collective-permute-start = (f32[4,64,128]{2,1,0:T(8,128)S(1)}, f32[4,64,128]{2,1,0:T(8,128)S(1)}, u32[]{:S(2)}, u32[]{:S(2)}) collective-permute-start(f32[4,64,128]{2,1,0:T(8,128)S(1)} %get-tuple-element.11.own_ref), channel_id=1, source_target_pairs={{0,8},{4,12},{8,16},{12,20},{16,24},{20,28},{24,32},{28,36},{32,40... | collective-permute-start | bytes 393224 | tf_op jit(solution)/shard_map/ppermute | solution.py:446
  5.1 0.0 copy-done
  5.1 6.6 %collective-permute-start.1 = (f32[2,64,128]{2,1,0:T(8,128)S(1)}, f32[2,64,128]{2,1,0:T(8,128)S(1)}, u32[]{:S(2)}, u32[]{:S(2)}) collective-permute-start(f32[2,64,128]{2,1,0:T(8,128)S(1)} %bitcast.19), channel_id=1, source_target_pairs={{0,4},{4,0},{8,12},{12,8},{16,20},{20,16},{24,28},{28,24},{32,36},... | collective-permute-start | bytes 196616 | tf_op jit(solution)/shard_map/ppermute | solution.py:447
  11.8 0.9 %collective-permute-done.1.across_ref = f32[2,64,128]{2,1,0:T(8,128)S(1)} collective-permute-done((f32[2,64,128]{2,1,0:T(8,128)S(1)}, f32[2,64,128]{2,1,0:T(8,128)S(1)}, u32[]{:S(2)}, u32[]{:S(2)}) %collective-permute-start.1) | collective-permute-done | bytes 65568 | tf_op jit(solution)/shard_map/ppermute | solution.py:447
  12.7 6.0 %collective-permute-done.before_ref = f32[4,64,128]{2,1,0:T(8,128)S(1)} collective-permute-done((f32[4,64,128]{2,1,0:T(8,128)S(1)}, f32[4,64,128]{2,1,0:T(8,128)S(1)}, u32[]{:S(2)}, u32[]{:S(2)}) %collective-permute-start) | collective-permute-done | bytes 131104 | tf_op jit(solution)/shard_map/ppermute | solution.py:446
  18.7 0.2 pair_sources.1
  18.9 10.2 %all_to_all.10.in_ref = f32[4,3,64,128]{3,2,1,0:T(8,128)S(1)} all-to-all(f32[4,3,64,128]{3,2,1,0:T(8,128)S(1)} %pair_sources.1), channel_id=1, replica_groups=mesh['orb'=128,'grid'=4] {'grid'}, dimensions={0} | all-to-all | bytes 786432 | tf_op jit(solution)/shard_map/all_to_all | solution.py:457
  29.0 3.8 %pair_solve.1 = f32[4,2,64,128]{3,2,1,0:T(8,128)S(1)} custom-call(f32[4,3,64,128]{3,2,1,0:T(8,128)S(1)} %all_to_all.10.in_ref), custom_call_target="tpu_custom_call" | custom-call | tf_op jit(solution)/shard_map/pair_solve/pallas_call | solution.py:460
  32.8 7.9 %all_to_all.11.pot_ref = f32[4,2,64,128]{3,2,1,0:T(8,128)S(1)} all-to-all(f32[4,2,64,128]{3,2,1,0:T(8,128)S(1)} %pair_solve.1), channel_id=1, replica_groups=mesh['orb'=128,'grid'=4] {'grid'}, dimensions={0} | all-to-all | bytes 524288 | tf_op jit(solution)/shard_map/all_to_all | solution.py:476
  40.7 0.3 pair_actions.1
  41.0 5.7 %collective-permute-start.2 = (f32[2,64,128]{2,1,0:T(8,128)S(1)}, f32[2,64,128]{2,1,0:T(8,128)S(1)}, u32[]{:S(2)}, u32[]{:S(2)}) collective-permute-start(f32[2,64,128]{2,1,0:T(8,128)S(1)} %get-tuple-element.13), channel_id=1, source_target_pairs={{0,4},{4,0},{8,12},{12,8},{16,20},{20,16},{24,28},{28,24},{32,36},... | collective-permute-start | bytes 196616 | tf_op jit(solution)/shard_map/ppermute | solution.py:491
  46.7 3.2 %collective-permute-start.3 = (f32[2,64,128]{2,1,0:T(8,128)S(1)}, f32[2,64,128]{2,1,0:T(8,128)S(1)}, u32[]{:S(2)}, u32[]{:S(2)}) collective-permute-start(f32[2,64,128]{2,1,0:T(8,128)S(1)} %get-tuple-element.14), channel_id=1, source_target_pairs={{0,504},{4,508},{8,0},{12,4},{16,8},{20,12},{24,16},{28,20},{32,24... | collective-permute-start | bytes 196616 | tf_op jit(solution)/shard_map/ppermute | solution.py:490
  50.0 0.0 collective-permute-done.2
  50.0 2.3 %collective-permute-done.3 = f32[2,64,128]{2,1,0:T(8,128)S(1)} collective-permute-done((f32[2,64,128]{2,1,0:T(8,128)S(1)}, f32[2,64,128]{2,1,0:T(8,128)S(1)}, u32[]{:S(2)}, u32[]{:S(2)}) %collective-permute-start.3) | collective-permute-done | bytes 65568 | tf_op jit(solution)/shard_map/ppermute | solution.py:490
  52.3 0.6 %add_bitcast_fusion = f32[2,8,1024]{2,1,0:T(8,128)} fusion(f32[2,64,128]{2,1,0:T(8,128)S(1)} %collective-permute-done.3, f32[2,64,128]{2,1,0:T(8,128)S(1)} %get-tuple-element.12, f32[2,64,128]{2,1,0:T(8,128)S(1)} %collective-permute-done.2), kind=kLoop, calls=%fused_computation | loop fusion | flops 32768 | bytes 262144 | tf_op jit(solution)/shard_map/reshape | solution.py:32
Async XLA Ops:
  0.0 5.1 %copy-start = (f32[2,8,1024]{2,1,0:T(8,128)S(1)}, f32[2,8,1024]{2,1,0:T(8,128)}, u32[]{:S(2)}) copy-start(f32[2,8,1024]{2,1,0:T(8,128)} %param.5) | copy-start | bytes 196612
  1.1 17.6 %collective-permute-start = (f32[4,64,128]{2,1,0:T(8,128)S(1)}, f32[4,64,128]{2,1,0:T(8,128)S(1)}, u32[]{:S(2)}, u32[]{:S(2)}) collective-permute-start(f32[4,64,128]{2,1,0:T(8,128)S(1)} %get-tuple-element.11.own_ref), channel_id=1, source_target_pairs={{0,8},{4,12},{8,16},{12,20},{16,24},{20,28},{24,32},{28,36},{32,40... | collective-permute-start | bytes 393224 | tf_op jit(solution)/shard_map/ppermute | solution.py:446
  5.1 7.5 %collective-permute-start.1 = (f32[2,64,128]{2,1,0:T(8,128)S(1)}, f32[2,64,128]{2,1,0:T(8,128)S(1)}, u32[]{:S(2)}, u32[]{:S(2)}) collective-permute-start(f32[2,64,128]{2,1,0:T(8,128)S(1)} %bitcast.19), channel_id=1, source_target_pairs={{0,4},{4,0},{8,12},{12,8},{16,20},{20,16},{24,28},{28,24},{32,36},... | collective-permute-start | bytes 196616 | tf_op jit(solution)/shard_map/ppermute | solution.py:447
  41.0 9.0 %collective-permute-start.2 = (f32[2,64,128]{2,1,0:T(8,128)S(1)}, f32[2,64,128]{2,1,0:T(8,128)S(1)}, u32[]{:S(2)}, u32[]{:S(2)}) collective-permute-start(f32[2,64,128]{2,1,0:T(8,128)S(1)} %get-tuple-element.13), channel_id=1, source_target_pairs={{0,4},{4,0},{8,12},{12,8},{16,20},{20,16},{24,28},{28,24},{32,36},... | collective-permute-start | bytes 196616 | tf_op jit(solution)/shard_map/ppermute | solution.py:491
  46.7 5.5 %collective-permute-start.3 = (f32[2,64,128]{2,1,0:T(8,128)S(1)}, f32[2,64,128]{2,1,0:T(8,128)S(1)}, u32[]{:S(2)}, u32[]{:S(2)}) collective-permute-start(f32[2,64,128]{2,1,0:T(8,128)S(1)} %get-tuple-element.14), channel_id=1, source_target_pairs={{0,504},{4,508},{8,0},{12,4},{16,8},{20,12},{24,16},{28,20},{32,24... | collective-permute-start | bytes 196616 | tf_op jit(solution)/shard_map/ppermute | solution.py:490
